TPU v7x, 256 devices: a whole 4x4x8 slice. The times are simulated.
256 devices in a mesh: wide: 128 (over y_lo, z, x, core), lev: 2 (over y_hi).
Axes of the slice: x: 4, y: 4 (y_hi: 2, y_lo: 2; y = y_hi * 2 + y_lo), z: 8, core: 2. Of those that a mesh axis runs over, the one named last changes fastest.
Arguments:
- member_control: float32 [128, 128, 128], P('wide'), may hold values from -6 to 6
- static_control: float32 [8, 1024, 1024], P('lev', 'wide'), may hold values from -6 to 6
- perturbations: bfloat16 [128, 8, 1024, 1024], P(None, 'lev', 'wide'), may hold values from -6 to 6
- innovation: float32 [8, 1024, 1024], P('lev', 'wide'), may hold values from -9 to 9
- diffusivity: float32 [8, 1024, 1024], P('lev', 'wide'), may hold values from 0.05 to 0.15
- rows_factor: float32 [128, 128], replicated, may hold values from -0.5 to 0.5
- column_factor: float32 [128, 128], replicated, may hold values from -0.5 to 0.5
- ocean_mask: int32 [1024, 1024], P('wide'), may hold values 0 or 1
- huber_blocks: int32 [8, 128, 128], P('lev', 'wide'), may hold values 0 or 1
- fold_map: int32 [1024], replicated, may hold values from 0 to 1023, as said below
Outputs:
- increment: float32 [8, 1024, 1024], P('lev', 'wide')
- member_gradient: float32 [128, 128, 128], P('wide')
- static_gradient: float32 [8, 1024, 1024], P('lev', 'wide')
Inputs may be any that keep to these rules, and one draw needn't show every extreme that they name: fold_map[fold_map[j]] = j and fold_map[j] != j for every column j.
All inputs are finite; a program needn't handle non-finite values. No bound on the sum of `ocean_mask` or of `huber_blocks` on one device may be relied on, other than what follows from the above.
Results may differ from a plain program's by a relative error of at most 0.0003.
Values sent between devices are 32-bit elements; how exact they have to be, the bound alone decides.
A program may use at most 64 MiB of HBM per device.

v0:
```python
import jax
import jax.numpy as jnp
from jax import lax
from jax.sharding import PartitionSpec as P

REFINE = 8
STEPS = 3


HUBER_EDGE = 1.0
VERTICAL_WEIGHT = 0.5
PRECISE = lax.Precision.HIGHEST


def with_halo(array, sides, width):
    for axis, dim in sides:
        count, length = (lax.axis_size(axis), array.shape[dim])
        up = [(i, (i + 1) % count) for i in range(count - 1)]
        down = [(j, i) for i, j in up]
        last = lax.slice_in_dim(array, length - width, length, axis=dim)
        first = lax.slice_in_dim(array, 0, width, axis=dim)
        before = lax.ppermute(last, axis, up)
        after = lax.ppermute(first, axis, down)
        array = jnp.concatenate([before, array, after], axis=dim)
    return array


def over_pieces(array, axis):
    return lax.all_gather(array, axis).sum(0)


def smooth_fields(values, rows_factor, column_factor):
    left_done = jnp.einsum("ij,mjk->mik", rows_factor, values, precision=PRECISE)
    return jnp.einsum("mik,kl->mil", left_done, column_factor, precision=PRECISE)


def smooth_adjoint(values, rows_factor, column_factor):
    left_done = jnp.einsum("ji,mjk->mik", rows_factor, values, precision=PRECISE)
    return jnp.einsum("mik,lk->mil", left_done, column_factor, precision=PRECISE)


def interpolate(extended, refine):
    fraction = jnp.arange(refine, dtype=jnp.float32) / refine
    below_row = extended[..., :-1, None, :]
    above_row = extended[..., 1:, None, :]
    row_terms = below_row * (1.0 - fraction)[:, None] + above_row * fraction[:, None]
    dims_of = row_terms.shape
    row_terms = row_terms.reshape(dims_of[:-3] + (dims_of[-3] * refine, dims_of[-1]))
    wrapped = jnp.roll(row_terms, -1, axis=-1)
    col_terms = row_terms[..., None] * (1.0 - fraction) + wrapped[..., None] * fraction
    return col_terms.reshape(row_terms.shape[:-1] + (row_terms.shape[-1] * refine,))


def interpolate_adjoint(fine_field, refine):
    fraction = jnp.arange(refine, dtype=jnp.float32) / refine
    dims_of = fine_field.shape
    col_terms = fine_field.reshape(dims_of[:-1] + (dims_of[-1] // refine, refine))
    coarse_cols = jnp.sum(col_terms * (1.0 - fraction), axis=-1) + jnp.roll(
        jnp.sum(col_terms * fraction, axis=-1), 1, axis=-1
    )
    row_terms = coarse_cols.reshape(
        dims_of[:-2] + (dims_of[-2] // refine, refine, dims_of[-1] // refine)
    )
    below_part = jnp.sum(row_terms * (1.0 - fraction)[:, None], axis=-2)
    above_part = jnp.sum(row_terms * fraction[:, None], axis=-2)
    zero_row = jnp.zeros_like(below_part)
    return jnp.concatenate([below_part, zero_row], axis=-2) + jnp.concatenate(
        [zero_row, above_part], axis=-2
    )


def stencil_update(values, root_kappa, scaled):
    padded = jnp.pad(scaled, ((1, 1), (1, 1), (0, 0)))
    across = (
        padded[1:-1, 2:, :]
        + padded[1:-1, :-2, :]
        + jnp.roll(scaled, 1, axis=2)
        + jnp.roll(scaled, -1, axis=2)
        - 4.0 * scaled
    )
    vertical = padded[2:, 1:-1, :] + padded[:-2, 1:-1, :] - 2.0 * scaled
    return values + root_kappa * (across + VERTICAL_WEIGHT * vertical)


def diffuse(values, diffusivity, fold_map):
    is_last = lax.axis_index("wide") == lax.axis_size("wide") - 1
    levels, rows = (values.shape[0], values.shape[1])
    stacked = jnp.stack([values, diffusivity], axis=0)
    extended = with_halo(stacked, (("wide", 2), ("lev", 1)), STEPS)
    field = extended[0]
    root_ext = jnp.sqrt(extended[1])
    fold_row = STEPS + rows
    for _ in range(STEPS):
        scaled = root_ext * field
        folded = jnp.take(scaled[:, fold_row - 1, :], fold_map, axis=1)
        scaled = scaled.at[:, fold_row, :].set(jnp.where(is_last, folded, scaled[:, fold_row, :]))
        field = stencil_update(field, root_ext, scaled)
    return field[STEPS : STEPS + levels, STEPS : STEPS + rows, :]


def huber_weigh(increment, innovation, ocean_cells, huber_blocks):
    misfit = increment - innovation
    expanded = jnp.repeat(jnp.repeat(huber_blocks, REFINE, axis=1), REFINE, axis=2)
    weight = jnp.where(expanded == 1, HUBER_EDGE / jnp.maximum(jnp.abs(misfit), HUBER_EDGE), 1.0)
    return ocean_cells * weight * misfit


def on_device(
    member_control,
    static_control,
    perturbations,
    innovation,
    diffusivity,
    rows_factor,
    column_factor,
    ocean_mask,
    huber_blocks,
    fold_map,
):
    members = perturbations.shape[0]
    member_scale = (members - 1) ** (-0.5)
    wide_count = lax.axis_size("wide")
    smoothed = smooth_fields(member_control, rows_factor, column_factor)
    held, coarse_rows, width = smoothed.shape
    tile_rows = coarse_rows // wide_count
    main_rows = smoothed.reshape(held, wide_count, tile_rows, width)
    next_rows = jnp.concatenate([smoothed[:, tile_rows::tile_rows, :], smoothed[:, -1:, :]], axis=1)
    windows = jnp.concatenate([main_rows, next_rows[:, :, None, :]], axis=2)
    arrived = lax.all_to_all(windows, "wide", split_axis=1, concat_axis=0, tiled=True)
    extended = arrived.reshape(members, tile_rows + 1, width)
    fine_field = interpolate(extended, REFINE)
    ensemble = jnp.sum(fine_field[:, None] * perturbations, axis=0)
    ocean_cells = ocean_mask.astype(jnp.float32)
    increment = ocean_cells * (
        member_scale * ensemble + diffuse(static_control, diffusivity, fold_map)
    )
    weighted = huber_weigh(increment, innovation, ocean_cells, huber_blocks)
    static_gradient = static_control + diffuse(weighted, diffusivity, fold_map)
    fine_terms = jnp.sum(perturbations * weighted[None], axis=1) * member_scale
    level_part = interpolate_adjoint(fine_terms, REFINE)
    ext_grad = over_pieces(level_part, "lev")
    windows = lax.all_to_all(ext_grad[:, None], "wide", split_axis=0, concat_axis=1, tiled=True)
    main_rows = windows[:, :, :tile_rows, :]
    next_rows = windows[:, :, tile_rows, :]
    main_rows = main_rows.at[:, 1:, 0, :].add(next_rows[:, :-1, :])
    main_rows = main_rows.at[:, -1, tile_rows - 1, :].add(next_rows[:, -1, :])
    smooth_grad = main_rows.reshape(held, coarse_rows, width)
    member_gradient = member_control + smooth_adjoint(smooth_grad, rows_factor, column_factor)
    return (increment, member_gradient, static_gradient)


def solution(mesh):
    return jax.shard_map(
        on_device,
        mesh=mesh,
        in_specs=(
            P("wide", None, None),
            P("lev", "wide", None),
            P(None, "lev", "wide", None),
            P("lev", "wide", None),
            P("lev", "wide", None),
            P(),
            P(),
            P("wide", None),
            P("lev", "wide", None),
            P(),
        ),
        out_specs=(P("lev", "wide", None), P("wide", None, None), P("lev", "wide", None)),
        check_vma=False,
    )
```

profile of v0, /device:TPU:24, one launch (start us, length us, event | category | flops | bytes accessed | tf_op | source)
XLA Modules:
  0.0 173.7 jit_solution(17829113664719446992)
XLA Ops:
  1.9 9.6 %collective-permute-start.1 = (f32[2,4,3,1024]{3,1,2,0:T(4,128)S(1)}, f32[2,4,3,1024]{3,1,2,0:T(4,128)S(1)}, u32[]{:S(2)}, u32[]{:S(2)}) collective-permute-start(f32[2,4,3,1024]{3,1,2,0:T(4,128)S(1)} %get-tuple-element.175), channel_id=1, source_target_pairs={{2,0},{4,2},{6,4},{8,6},{10,8},{12,10},{14,12},{16,14},{18,16},{20... | collective-permute-start | bytes 294920 | tf_op jit(solution)/shard_map/ppermute | solution.py:23
  11.5 1.9 %collective-permute-start = (f32[2,4,3,1024]{3,1,2,0:T(4,128)S(1)}, f32[2,4,3,1024]{3,1,2,0:T(4,128)S(1)}, u32[]{:S(2)}, u32[]{:S(2)}) collective-permute-start(f32[2,4,3,1024]{3,1,2,0:T(4,128)S(1)} %get-tuple-element.174), channel_id=1, source_target_pairs={{0,2},{2,4},{4,6},{6,8},{8,10},{10,12},{12,14},{14,16},{16,18},{18... | collective-permute-start | bytes 294920 | tf_op jit(solution)/shard_map/ppermute | solution.py:22
  16.5 9.4 %all-to-all-start = ((f32[1,128,2,128]{3,2,0,1:T(2,128)}), f32[1,128,2,128]{3,2,0,1:T(2,128)S(1)}, u32[]{:S(2)}, u32[]{:S(2)}) async-start(f32[1,128,2,128]{3,2,0,1:T(2,128)} %copy.297), calls=%async_computation | async-start | bytes 262144 | tf_op jit(solution)/shard_map/all_to_all | solution.py:129
  29.2 3.1 %collective-permute-start.3 = (f32[2,3,14,1024]{3,0,2,1:T(2,128)S(1)}, f32[2,3,14,1024]{3,0,2,1:T(2,128)S(1)}, u32[]{:S(2)}, u32[]{:S(2)}) collective-permute-start(f32[2,3,14,1024]{3,0,2,1:T(2,128)S(1)} %copy.304), channel_id=1, source_target_pairs={{1,0},{3,2},{5,4},{7,6},{9,8},{11,10},{13,12},{15,14},{17,16},{19,... | collective-permute-start | bytes 1032200 | tf_op jit(solution)/shard_map/ppermute | solution.py:23
  32.6 1.5 collective-permute-start.2
  34.0 3.0 %all-to-all-done = f32[1,128,2,128]{3,2,0,1:T(2,128)S(1)} async-done(((f32[1,128,2,128]{3,2,0,1:T(2,128)}), f32[1,128,2,128]{3,2,0,1:T(2,128)S(1)}, u32[]{:S(2)}, u32[]{:S(2)}) %all-to-all-start) | async-done | bytes 131104 | tf_op jit(solution)/shard_map/all_to_all | solution.py:129
  37.6 2.4 %fusion.4 = f32[128,8,1024]{0,2,1:T(8,128)} fusion(f32[1024]{0:T(1024)S(1)} %mul.286, f32[128,8,128]{0,2,1:T(8,128)S(1)} %pad_maximum_fusion.2, f32[1024]{0:T(1024)S(1)} %mul.280, f32[128,8,128]{0,2,1:T(8,128)S(1)} %multiply_add_fusion), kind=kLoop, calls=%fused_computation.15 | loop fusion | flops 3145728 | bytes 5251072 | tf_op jit(solution)/shard_map/add | solution.py:50
  40.0 5.5 %copy.300 = f32[128,8,1024]{2,1,0:T(8,128)} copy(f32[128,8,1024]{0,2,1:T(8,128)} %fusion.4) | data formatting | bytes 8388608 | tf_op jit(solution)/shard_map/add | solution.py:50
  45.5 7.8 %fusion = f32[4,8,1024]{2,1,0:T(8,128)} fusion(bf16[128,4,8,1024]{3,2,1,0:T(8,128)(2,1)} %param.30, f32[128,8,1024]{2,1,0:T(8,128)} %copy.300), kind=kLoop, calls=%fused_computation.8 | loop fusion | flops 12550144 | bytes 12713984 | tf_op jit(solution)/shard_map/reduce_sum | solution.py:132
  54.8 4.0 %gather_fusion = f32[1024,10]{1,0:T(8,128)} fusion(f32[10,1024]{0,1:T(8,128)S(1)} %copy.307, s32[1024]{0:T(1024)S(1)} %fusion.89), kind=kCustom, calls=%fused_computation.clone | custom fusion | bytes 86016 | tf_op jit(solution)/shard_map/jit(_take)/gather | solution.py:95
  58.8 1.2 copy.308
  61.0 4.6 %fusion.95 = (f32[10,14,1024]{2,0,1:T(8,128)S(1)}, f32[10,14,1024]{2,0,1:T(8,128)}) fusion(f32[2,10,14,1024]{3,1,2,0:T(8,128)S(1)} %pad_maximum_fusion, f32[10,14,1024]{2,0,1:T(8,128)} %copy-done.2, f32[10,14,1]{2,0,1:T(8,128)S(1)} %get-tuple-element.146, f32[10,14,1023]{2,0,1:T(8,128)S(1)} %get-tuple-element.148, ...), kind=kLoop, calls=%fused_computation.190 | loop fusion | flops 2150400 | bytes 4014080 | tf_op jit(solution)/shard_map/mul | solution.py:94
  65.8 4.0 %gather_fusion.1 = f32[1024,10]{1,0:T(8,128)} fusion(f32[10,1024]{0,1:T(8,128)S(1)} %copy.312, s32[1024]{0:T(1024)S(1)} %fusion.89), kind=kCustom, calls=%fused_computation.1.clone | custom fusion | bytes 86016 | tf_op jit(solution)/shard_map/jit(_take)/gather | solution.py:95
  72.6 4.6 %fusion.94 = (f32[10,14,1024]{2,0,1:T(8,128)S(1)}, f32[10,14,1024]{2,0,1:T(8,128)}) fusion(f32[2,10,14,1024]{3,1,2,0:T(8,128)S(1)} %pad_maximum_fusion, f32[10,14,1024]{2,0,1:T(8,128)S(1)} %copy-done.3, f32[10,14,1024]{2,0,1:T(8,128)} %copy-done.1, f32[10,14,1]{2,0,1:T(8,128)S(1)} %get-tuple-element.142, f32[10,14,1023]{2,0,1:T(8,128)S(1)} %get-tuple-element.144, ...), kind=kLoop, calls=%fused_computation.189 | loop fusion | flops 2150400 | bytes 4014080 | tf_op jit(solution)/shard_map/mul | solution.py:94
  77.5 4.0 %gather_fusion.2 = f32[1024,10]{1,0:T(8,128)} fusion(f32[10,1024]{0,1:T(8,128)S(1)} %copy.317, s32[1024]{0:T(1024)S(1)} %fusion.89), kind=kCustom, calls=%fused_computation.2.clone | custom fusion | bytes 86016 | tf_op jit(solution)/shard_map/jit(_take)/gather | solution.py:95
  83.8 1.3 fusion.67
  85.9 8.7 %fusion.1 = f32[128,8,1024]{2,1,0:T(8,128)} fusion(bf16[128,4,8,1024]{3,2,1,0:T(8,128)(2,1)} %param.30, f32[4,8,1024]{2,1,0:T(8,128)S(1)} %get-tuple-element.126), kind=kLoop, calls=%fused_computation.9 | loop fusion | flops 11534336 | bytes 12713984 | tf_op jit(solution)/shard_map/reduce_sum | solution.py:139
  94.5 5.4 %copy.323 = f32[128,8,1024]{0,2,1:T(8,128)} copy(f32[128,8,1024]{2,1,0:T(8,128)} %fusion.1) | data formatting | bytes 8388608 | tf_op jit(solution)/shard_map/reduce_sum | solution.py:139
  99.9 5.0 %fusion.3 = (f32[128,8,128]{0,2,1:T(8,128)S(1)}, f32[128,8,128]{0,2,1:T(8,128)S(1)}) fusion(f32[128,8,1024]{0,2,1:T(8,128)} %copy.323, f32[8]{0:T(128)S(1)} %copy-done.18, f32[8]{0:T(128)S(1)} %copy-done.19), kind=kLoop, calls=%fused_computation.13 | loop fusion | flops 3932160 | bytes 5242944 | tf_op jit(solution)/shard_map/reduce_sum | solution.py:59
  105.1 3.0 %collective-permute-start.5 = (f32[2,4,3,1024]{3,1,2,0:T(4,128)S(1)}, f32[2,4,3,1024]{3,1,2,0:T(4,128)S(1)}, u32[]{:S(2)}, u32[]{:S(2)}) collective-permute-start(f32[2,4,3,1024]{3,1,2,0:T(4,128)S(1)} %copy.329), channel_id=1, source_target_pairs={{2,0},{4,2},{6,4},{8,6},{10,8},{12,10},{14,12},{16,14},{18,16},{20... | collective-permute-start | bytes 294920 | tf_op jit(solution)/shard_map/ppermute | solution.py:23
  108.2 1.9 %collective-permute-start.4 = (f32[2,4,3,1024]{3,1,2,0:T(4,128)S(1)}, f32[2,4,3,1024]{3,1,2,0:T(4,128)S(1)}, u32[]{:S(2)}, u32[]{:S(2)}) collective-permute-start(f32[2,4,3,1024]{3,1,2,0:T(4,128)S(1)} %copy.328), channel_id=1, source_target_pairs={{0,2},{2,4},{4,6},{6,8},{8,10},{10,12},{12,14},{14,16},{16,18},{18... | collective-permute-start | bytes 294920 | tf_op jit(solution)/shard_map/ppermute | solution.py:22
  110.3 7.9 %all-gather = f32[256,2,128]{0,2,1:T(8,128)S(1)} all-gather(f32[128,2,128]{0,2,1:T(8,128)S(1)} %pad_add_fusion), channel_id=2, replica_groups=mesh['wide'=128,'lev'=2] {'lev'}, dimensions={0}, use_global_device_ids=true | all-gather | bytes 393216 | tf_op jit(solution)/shard_map/all_gather | solution.py:29
  119.4 10.1 %all-to-all-start.1 = ((f32[128,1,2,128]{3,2,1,0:T(2,128)}), f32[128,1,2,128]{3,2,1,0:T(2,128)S(1)}, u32[]{:S(2)}, u32[]{:S(2)}) async-start(f32[128,1,2,128]{3,2,1,0:T(2,128)} %copy.324), calls=%async_computation.1 | async-start | bytes 262144 | tf_op jit(solution)/shard_map/all_to_all | solution.py:142
  130.2 5.6 %collective-permute-start.7 = (f32[2,3,14,1024]{3,0,2,1:T(2,128)S(1)}, f32[2,3,14,1024]{3,0,2,1:T(2,128)S(1)}, u32[]{:S(2)}, u32[]{:S(2)}) collective-permute-start(f32[2,3,14,1024]{3,0,2,1:T(2,128)S(1)} %copy.333), channel_id=1, source_target_pairs={{1,0},{3,2},{5,4},{7,6},{9,8},{11,10},{13,12},{15,14},{17,16},{19,... | collective-permute-start | bytes 1032200 | tf_op jit(solution)/shard_map/ppermute | solution.py:23
  136.1 1.3 collective-permute-start.6
  137.4 3.2 %all-to-all-done.1 = f32[128,1,2,128]{3,2,1,0:T(2,128)S(1)} async-done(((f32[128,1,2,128]{3,2,1,0:T(2,128)}), f32[128,1,2,128]{3,2,1,0:T(2,128)S(1)}, u32[]{:S(2)}, u32[]{:S(2)}) %all-to-all-start.1) | async-done | bytes 131104 | tf_op jit(solution)/shard_map/all_to_all | solution.py:142
  143.5 5.8 %collective-permute-done.6 = f32[2,3,14,1024]{3,0,2,1:T(2,128)S(1)} collective-permute-done((f32[2,3,14,1024]{3,0,2,1:T(2,128)S(1)}, f32[2,3,14,1024]{3,0,2,1:T(2,128)S(1)}, u32[]{:S(2)}, u32[]{:S(2)}) %collective-permute-start.6) | collective-permute-done | bytes 344096 | tf_op jit(solution)/shard_map/ppermute | solution.py:22
  152.0 4.0 %gather_fusion.3 = f32[1024,10]{1,0:T(8,128)} fusion(f32[10,1024]{0,1:T(8,128)S(1)} %copy.338, s32[1024]{0:T(1024)S(1)} %fusion.89), kind=kCustom, calls=%fused_computation.3.clone | custom fusion | bytes 86016 | tf_op jit(solution)/shard_map/jit(_take)/gather | solution.py:95
  159.0 4.0 %gather_fusion.4 = f32[1024,10]{1,0:T(8,128)} fusion(f32[10,1024]{0,1:T(8,128)S(1)} %bitcast.206, s32[1024]{0:T(1024)S(1)} %fusion.89), kind=kCustom, calls=%fused_computation.4.clone | custom fusion | bytes 86016 | tf_op jit(solution)/shard_map/jit(_take)/gather | solution.py:95
  165.2 1.5 fusion.92
  166.9 2.8 %gather_fusion.5 = f32[1024,10]{1,0:T(8,128)S(1)} fusion(f32[10,1024]{0,1:T(8,128)S(1)} %bitcast.205, s32[1024]{0:T(1024)S(1)} %fusion.89), kind=kCustom, calls=%fused_computation.5.clone | custom fusion | bytes 86016 | tf_op jit(solution)/shard_map/jit(_take)/gather | solution.py:95
  171.8 1.9 %fusion.60 = f32[4,8,1024]{2,1,0:T(8,128)} fusion(f32[4,8,1024]{2,1,0:T(8,128)S(1)} %copy-done.6, f32[10,14,1]{2,1,0:T(8,128)S(1)} %get-tuple-element.155, f32[10,14,1023]{2,1,0:T(8,128)S(1)} %get-tuple-element.153, f32[10,14,1024]{2,1,0:T(8,128)} %get-tuple-element.123, f32[10,14,1024]{2,1,0:T(8,128)} %copy-done.4, ...), kind=kLoop, calls=%fused_computation.118 | loop fusion | flops 458752 | bytes 2195456 | tf_op jit(solution)/shard_map/add | solution.py:138
  (162 shorter events, 32.0 us)
Async XLA Ops:
  0.6 12.8 %copy-start = (f32[128,128]{1,0:T(8,128)S(1)}, f32[128,128]{1,0:T(8,128)}, u32[]{:S(2)}) copy-start(f32[128,128]{1,0:T(8,128)} %param.33) | copy-start | bytes 196612
  0.6 25.3 %copy-start.14 = (s32[1024]{0:T(1024)S(1)}, s32[1024]{0:T(1024)}, u32[]{:S(2)}) copy-start(s32[1024]{0:T(1024)} %param.37) | copy-start | bytes 12292
  0.7 25.5 %copy-start.13 = (s32[8,1024]{1,0:T(8,128)S(1)}, s32[8,1024]{1,0:T(8,128)}, u32[]{:S(2)}) copy-start(s32[8,1024]{1,0:T(8,128)} %param.35) | copy-start | bytes 98308
  0.7 26.1 %copy-start.17 = (s32[4,1,128]{2,1,0:T(1,128)S(1)}, s32[4,1,128]{2,1,0:T(1,128)}, u32[]{:S(2)}) copy-start(s32[4,1,128]{2,1,0:T(1,128)} %param.36) | copy-start | bytes 6148
  1.9 25.9 %collective-permute-start.1 = (f32[2,4,3,1024]{3,1,2,0:T(4,128)S(1)}, f32[2,4,3,1024]{3,1,2,0:T(4,128)S(1)}, u32[]{:S(2)}, u32[]{:S(2)}) collective-permute-start(f32[2,4,3,1024]{3,1,2,0:T(4,128)S(1)} %get-tuple-element.175), channel_id=1, source_target_pairs={{2,0},{4,2},{6,4},{8,6},{10,8},{12,10},{14,12},{16,14},{18,16},{20... | collective-permute-start | bytes 294920 | tf_op jit(solution)/shard_map/ppermute | solution.py:23
  11.5 16.4 %collective-permute-start = (f32[2,4,3,1024]{3,1,2,0:T(4,128)S(1)}, f32[2,4,3,1024]{3,1,2,0:T(4,128)S(1)}, u32[]{:S(2)}, u32[]{:S(2)}) collective-permute-start(f32[2,4,3,1024]{3,1,2,0:T(4,128)S(1)} %get-tuple-element.174), channel_id=1, source_target_pairs={{0,2},{2,4},{4,6},{6,8},{8,10},{10,12},{12,14},{14,16},{16,18},{18... | collective-permute-start | bytes 294920 | tf_op jit(solution)/shard_map/ppermute | solution.py:22
  16.5 20.5 %all-to-all-start = ((f32[1,128,2,128]{3,2,0,1:T(2,128)}), f32[1,128,2,128]{3,2,0,1:T(2,128)S(1)}, u32[]{:S(2)}, u32[]{:S(2)}) async-start(f32[1,128,2,128]{3,2,0,1:T(2,128)} %copy.297), calls=%async_computation | async-start | bytes 262144 | tf_op jit(solution)/shard_map/all_to_all | solution.py:129
  26.0 11.3 %copy-start.15 = (f32[8]{0:T(128)}, f32[8]{0:T(128)S(1)}, u32[]{:S(2)}) copy-start(f32[8]{0:T(128)S(1)} %get-tuple-element.183) | copy-start | bytes 100
  27.9 0.6 copy-start.7
  29.2 24.1 %collective-permute-start.3 = (f32[2,3,14,1024]{3,0,2,1:T(2,128)S(1)}, f32[2,3,14,1024]{3,0,2,1:T(2,128)S(1)}, u32[]{:S(2)}, u32[]{:S(2)}) collective-permute-start(f32[2,3,14,1024]{3,0,2,1:T(2,128)S(1)} %copy.304), channel_id=1, source_target_pairs={{1,0},{3,2},{5,4},{7,6},{9,8},{11,10},{13,12},{15,14},{17,16},{19,... | collective-permute-start | bytes 1032200 | tf_op jit(solution)/shard_map/ppermute | solution.py:23
  32.6 21.0 %collective-permute-start.2 = (f32[2,3,14,1024]{3,0,2,1:T(2,128)S(1)}, f32[2,3,14,1024]{3,0,2,1:T(2,128)S(1)}, u32[]{:S(2)}, u32[]{:S(2)}) collective-permute-start(f32[2,3,14,1024]{3,0,2,1:T(2,128)S(1)} %copy.303), channel_id=1, source_target_pairs={{0,1},{2,3},{4,5},{6,7},{8,9},{10,11},{12,13},{14,15},{16,17},{18,... | collective-permute-start | bytes 1032200 | tf_op jit(solution)/shard_map/ppermute | solution.py:22
  45.5 8.3 %copy-start.8 = (f32[2,4,3,1024]{3,1,2,0:T(4,128)S(1)}, f32[2,4,3,1024]{3,1,2,0:T(4,128)}, u32[]{:S(2)}) copy-start(f32[2,4,3,1024]{3,1,2,0:T(4,128)} %copy-done.7) | copy-start | bytes 294916
  60.1 0.9 copy-start.2
  71.1 0.9 copy-start.1
  71.2 1.4 copy-start.3
  83.8 1.3 copy-start.5
  83.8 1.3 copy-start.11
  83.8 1.3 copy-start.12
  94.5 5.4 %copy-start.18 = (f32[8]{0:T(128)S(1)}, f32[8]{0:T(128)}, u32[]{:S(2)}) copy-start(f32[8]{0:T(128)} %get-tuple-element.184) | copy-start | bytes 100
  94.5 5.4 %copy-start.19 = (f32[8]{0:T(128)S(1)}, f32[8]{0:T(128)}, u32[]{:S(2)}) copy-start(f32[8]{0:T(128)} %get-tuple-element.185) | copy-start | bytes 100
  99.9 10.2 %copy-start.16 = (f32[8]{0:T(128)S(1)}, f32[8]{0:T(128)}, u32[]{:S(2)}) copy-start(f32[8]{0:T(128)} %copy-done.15) | copy-start | bytes 100
  105.1 24.4 %collective-permute-start.5 = (f32[2,4,3,1024]{3,1,2,0:T(4,128)S(1)}, f32[2,4,3,1024]{3,1,2,0:T(4,128)S(1)}, u32[]{:S(2)}, u32[]{:S(2)}) collective-permute-start(f32[2,4,3,1024]{3,1,2,0:T(4,128)S(1)} %copy.329), channel_id=1, source_target_pairs={{2,0},{4,2},{6,4},{8,6},{10,8},{12,10},{14,12},{16,14},{18,16},{20... | collective-permute-start | bytes 294920 | tf_op jit(solution)/shard_map/ppermute | solution.py:23
  108.2 21.4 %collective-permute-start.4 = (f32[2,4,3,1024]{3,1,2,0:T(4,128)S(1)}, f32[2,4,3,1024]{3,1,2,0:T(4,128)S(1)}, u32[]{:S(2)}, u32[]{:S(2)}) collective-permute-start(f32[2,4,3,1024]{3,1,2,0:T(4,128)S(1)} %copy.328), channel_id=1, source_target_pairs={{0,2},{2,4},{4,6},{6,8},{8,10},{10,12},{12,14},{14,16},{16,18},{18... | collective-permute-start | bytes 294920 | tf_op jit(solution)/shard_map/ppermute | solution.py:22
  119.4 21.1 %all-to-all-start.1 = ((f32[128,1,2,128]{3,2,1,0:T(2,128)}), f32[128,1,2,128]{3,2,1,0:T(2,128)S(1)}, u32[]{:S(2)}, u32[]{:S(2)}) async-start(f32[128,1,2,128]{3,2,1,0:T(2,128)} %copy.324), calls=%async_computation.1 | async-start | bytes 262144 | tf_op jit(solution)/shard_map/all_to_all | solution.py:142
  129.8 11.6 %copy-start.9 = (f32[1,128,128]{2,1,0:T(8,128)S(1)}, f32[1,128,128]{2,1,0:T(8,128)}, u32[]{:S(2)}) copy-start(f32[1,128,128]{2,1,0:T(8,128)} %param.28) | copy-start | bytes 196612
  129.8 11.6 %copy-start.10 = (f32[128,128]{1,0:T(8,128)S(1)}, f32[128,128]{1,0:T(8,128)}, u32[]{:S(2)}) copy-start(f32[128,128]{1,0:T(8,128)} %param.34) | copy-start | bytes 196612
  130.2 13.2 %collective-permute-start.7 = (f32[2,3,14,1024]{3,0,2,1:T(2,128)S(1)}, f32[2,3,14,1024]{3,0,2,1:T(2,128)S(1)}, u32[]{:S(2)}, u32[]{:S(2)}) collective-permute-start(f32[2,3,14,1024]{3,0,2,1:T(2,128)S(1)} %copy.333), channel_id=1, source_target_pairs={{1,0},{3,2},{5,4},{7,6},{9,8},{11,10},{13,12},{15,14},{17,16},{19,... | collective-permute-start | bytes 1032200 | tf_op jit(solution)/shard_map/ppermute | solution.py:23
  136.1 13.3 %collective-permute-start.6 = (f32[2,3,14,1024]{3,0,2,1:T(2,128)S(1)}, f32[2,3,14,1024]{3,0,2,1:T(2,128)S(1)}, u32[]{:S(2)}, u32[]{:S(2)}) collective-permute-start(f32[2,3,14,1024]{3,0,2,1:T(2,128)S(1)} %copy.332), channel_id=1, source_target_pairs={{0,1},{2,3},{4,5},{6,7},{8,9},{10,11},{12,13},{14,15},{16,17},{18,... | collective-permute-start | bytes 1032200 | tf_op jit(solution)/shard_map/ppermute | solution.py:22
  149.9 0.8 copy-start.4
  170.9 0.9 copy-start.6
where the time goes:
time: 175 us; the launch traced here: 174 us
  local copies, waits for them, and re-layouts  56.6 us (32%)
  starting transfers between devices  47.4 us (27%)
  other arithmetic  43.6 us (25%)
  waiting for transfers between devices  13.1 us (7%)
  blocking collectives  7.94 us (5%)
  matrix products  3.45 us (2%)
    gather x12, local copies, waits for them, and re-layouts, diffuse(): folded = jnp.take(scaled[:, fold_row - 1, :], fold_map, axis=1)  29.2 us
    ppermute x4, starting transfers between devices, with_halo(): after = lax.ppermute(first, axis, down)  21.3 us
    mul x6, other arithmetic, diffuse(): scaled = root_ext * field  12.2 us
    all_to_all x1, starting transfers between devices, on_device(): lax.all_to_all(ext_grad[:, None], 'wide', split_axis=0, concat_axis=1, ti...  10.1 us
    all_to_all x1, starting transfers between devices, on_device(): lax.all_to_all(windows, 'wide', split_axis=1, concat_axis=0, tiled=True)  9.45 us
    reduce_sum x1, other arithmetic, on_device(): fine_terms = jnp.sum(perturbations * weighted[None], axis=1) * member_scale  8.66 us
    all_gather x1, blocking collectives, over_pieces(): return lax.all_gather(array, axis).sum(0)  7.94 us
    reduce_sum x1, other arithmetic, on_device(): ensemble = jnp.sum(fine_field[:, None] * perturbations, axis=0)  7.76 us
  transfers between devices with their start and end apart: 10, of which 4 were waited for; matrix products, arithmetic and copies ran while one was open for 15% of the time, Pallas kernels for 0%

commit v1 on v0

v1 whole, which is shorter than its diff:
```python
import functools

import jax
import jax.numpy as jnp
from jax import lax
from jax.experimental import pallas as pl
from jax.experimental.pallas import tpu as pltpu
from jax.sharding import PartitionSpec as P

STEPS = 3
WIDE = 128
GROUP = 16
GROUPS = WIDE // GROUP
LEVELS = 4
TILES = 8
F32 = jnp.float32
BF16 = jnp.bfloat16
MESH = pl.DeviceIdType.MESH
PRECISE = lax.Precision.HIGHEST
SCALE = 127.0 ** (-0.5)
OWN = LEVELS * 64
HALO = STEPS * 64
ALL_ROWS = (8 + 2 * STEPS) * 64


def rows_at(start, size, step=1):
    if step == 1:
        return pl.ds(pl.multiple_of(start, 8), size)
    return pl.ds(start, size, stride=step)


def kernel(
    mc_hbm, sc_hbm, pert_hbm, inn_hbm, dif_hbm, rf_hbm, cf_hbm, mask_hbm, hub_hbm, fold_hbm,
    inc_hbm, mg_hbm, sg_hbm,
    pert, mc, cf, r2, win, ext, bb, sb, nat_s, nat_k, nat_w, inn, mask, hub, fold,
    v_s, v_w, kap, s_buf, tmp, ww, wt, lhs, fbuf, gbuf, ens, wsc, hubx, incb, sgb, mgb,
    load_sem, out_sem, fwd_send, fwd_recv, bwd_send, bwd_recv, lev_send, lev_recv, row_send, row_recv,
):
    w = lax.axis_index("wide")
    lev = lax.axis_index("lev")
    group, place = w // GROUP, w % GROUP
    right, left = (w + 1) % WIDE, (w + WIDE - 1) % WIDE
    own0 = pl.multiple_of(lev * OWN, OWN)

    def remote(src, dst, send, recv, wide=None, level=None):
        target = {"wide": w if wide is None else wide, "lev": lev if level is None else level}
        return pltpu.make_async_remote_copy(
            src_ref=src, dst_ref=dst, send_sem=send, recv_sem=recv, device_id=target, device_id_type=MESH
        )

    def wait_bytes(ref, sem):
        pltpu.make_async_copy(ref, ref, sem).wait()

    barrier = pltpu.get_barrier_semaphore()

    def tell(i, _):
        pl.semaphore_signal(barrier, inc=1, device_id={"wide": (w + i) % WIDE, "lev": lev}, device_id_type=MESH)
        return _

    lax.fori_loop(1, WIDE, tell, 0)
    pl.semaphore_signal(barrier, inc=1, device_id={"wide": w, "lev": 1 - lev}, device_id_type=MESH)

    loads = [
        (mc_hbm, mc), (cf_hbm, cf), (rf_hbm, tmp.at[pl.ds(0, 128)]),
        (sc_hbm, nat_s.at[pl.ds(own0, OWN)]), (dif_hbm, nat_k.at[pl.ds(own0, OWN)]),
        (pert_hbm, pert), (inn_hbm, inn), (mask_hbm, mask), (hub_hbm, hub.at[pl.ds(0, LEVELS)]), (fold_hbm, fold),
    ]
    loads = [pltpu.make_async_copy(src, dst, load_sem.at[i]) for i, (src, dst) in enumerate(loads)]
    for load in loads:
        load.start()

    j = lax.broadcasted_iota(jnp.int32, (WIDE, 1024), 0)
    x = lax.broadcasted_iota(jnp.int32, (WIDE, 1024), 1)
    part = (x % 8).astype(F32) * 0.125
    weights = jnp.where(x // 8 == j, 1.0 - part, 0.0) + jnp.where((x // 8 + 1) % WIDE == j, part, 0.0)
    ww[0:128] = weights.astype(BF16)
    ww[128:256] = weights.astype(BF16)
    x = lax.broadcasted_iota(jnp.int32, (1024, WIDE), 0)
    j = lax.broadcasted_iota(jnp.int32, (1024, WIDE), 1)
    part = (x % 8).astype(F32) * 0.125
    weights = jnp.where(x // 8 == j, 1.0 - part, 0.0) + jnp.where((x // 8 + 1) % WIDE == j, part, 0.0)
    wt[...] = weights.astype(BF16)

    for i in range(3):
        loads[i].wait()
    r2[pl.ds(0, 128, stride=2), :] = tmp[0:128]
    r2[pl.ds(1, 128, stride=2), :] = jnp.concatenate([tmp[1:128], tmp[127:128]], axis=0)
    columns_done = jnp.dot(mc[...], cf[...], precision=PRECISE, preferred_element_type=F32)
    win[...] = jnp.dot(r2[...], columns_done, precision=PRECISE, preferred_element_type=F32)

    pl.semaphore_wait(barrier, WIDE)

    def offset_of(n):
        return 4 + (1 - 2 * (n % 2)) * ((n + 1) // 2)

    def send_window(n, _):
        i = offset_of(n // GROUP)
        to = ((group + i) % GROUPS) * GROUP + (place + n % GROUP) % GROUP
        remote(win.at[pl.ds(2 * to, 2)], ext.at[pl.ds(2 * w, 2)], fwd_send, fwd_recv.at[i], wide=to).start()
        return _

    lax.fori_loop(0, 7 * GROUP, send_window, 0)
    lax.fori_loop(7 * GROUP + 1, 8 * GROUP, send_window, 0)
    pltpu.make_async_copy(win.at[pl.ds(2 * w, 2)], ext.at[pl.ds(2 * w, 2)], fwd_recv.at[0]).start()

    for i in (3, 4):
        loads[i].wait()
    seen = pl.ds(pl.multiple_of(64 + 192 * lev, 64), 192)
    unseen = pl.ds(pl.multiple_of(448 * (1 - lev), 64), 64)
    lev_copies = [
        remote(nat.at[seen], nat.at[seen], lev_send.at[i], lev_recv.at[i], level=1 - lev)
        for i, nat in enumerate((nat_s, nat_k, nat_w))
    ]
    lev_copies[0].start()
    lev_copies[1].start()
    for nat in (nat_s, nat_k, nat_w):
        nat[unseen, :] = jnp.zeros((64, 128), F32)

    def to_rows(nat, out, change):
        def body(r, _):
            for t in range(TILES):
                out[rows_at((r + STEPS) * 64 + t * 8, 8), :] = change(nat[rows_at(t * 8 + r, 8, 64), :])
            return _

        lax.fori_loop(0, 8, body, 0)

    def to_natural(rows, out):
        def body(r, _):
            for t in range(TILES):
                out[rows_at(t * 8 + r, 8, 64), :] = rows[rows_at((r + STEPS) * 64 + t * 8, 8), :]
            return _

        lax.fori_loop(0, 8, body, 0)

    def row_copies(rows, i):
        down = remote(rows.at[pl.ds(8 * 64, HALO)], rows.at[pl.ds(0, HALO)], row_send.at[i], row_recv.at[i], wide=right)
        up = remote(
            rows.at[pl.ds(3 * 64, HALO)], rows.at[pl.ds(11 * 64, HALO)], row_send.at[i + 1], row_recv.at[i + 1], wide=left
        )
        return [down, up]

    static_rows = row_copies(v_s, 0) + row_copies(kap, 2)
    weighted_rows = row_copies(v_w, 4)

    sublane = lax.broadcasted_iota(jnp.int32, (8, 8, 128), 1)
    lane = lax.broadcasted_iota(jnp.int32, (64, 128), 1)

    def fold_row(row):
        def body(t, _):
            entry = jnp.broadcast_to(fold[pl.ds(t, 1), :], (8, 128))
            at, tile = entry % 128, entry // 128
            total = jnp.zeros((8, 128), F32)
            for u in range(TILES):
                there = jnp.take_along_axis(s_buf[pl.ds(row * 64 + u * 8, 8), :], at, axis=1)
                total = jnp.where(tile == u, there, total)
            here = rows_at((row + 1) * 64 + t * 8, 8)
            s_buf[here, :] = jnp.where(w == WIDE - 1, total, s_buf[here, :])
            return _

        lax.fori_loop(0, TILES, body, 0)

    def diffuse(v):
        for step in range(1, STEPS + 1):
            def scale_row(i, _):
                here = rows_at(i * 64, 64)
                s_buf[here, :] = kap[here, :] * v[here, :]
                return _

            lax.fori_loop(step - 1, 8 + 2 * STEPS + 1 - step, scale_row, 0)
            fold_row(STEPS + 7)

            def update_row(i, _):
                here = rows_at(i * 64, 64)
                s = s_buf[here, :]
                after = pltpu.roll(s, 1, 1)
                before = pltpu.roll(s, 127, 1)
                west = jnp.where(lane == 0, jnp.concatenate([after[56:], after[:56]], axis=0), after)
                east = jnp.where(lane == 127, jnp.concatenate([before[8:], before[:8]], axis=0), before)
                s3 = s.reshape(8, 8, 128)
                below = jnp.where(sublane == 0, 0.0, pltpu.roll(s3, 1, 1)).reshape(64, 128)
                above = jnp.where(sublane == 7, 0.0, pltpu.roll(s3, 7, 1)).reshape(64, 128)
                across = s_buf[rows_at(i * 64 + 64, 64), :] + s_buf[rows_at(i * 64 - 64, 64), :] + west + east
                v[here, :] = v[here, :] + kap[here, :] * (across + 0.5 * (below + above) - 5.0 * s)
                return _

            lax.fori_loop(step, 8 + 2 * STEPS - step, update_row, 0)

    eighth = lax.broadcasted_iota(jnp.int32, (8, 128), 0).astype(F32) * 0.125
    loads[5].wait()
    ens[...] = jnp.zeros((LEVELS, 8, 1024), F32)

    def ensemble_group(n, _):
        i = offset_of(7 - n)
        first = ((group + GROUPS - i) % GROUPS) * GROUP
        wait_bytes(ext.at[pl.ds(0, 2 * GROUP)], fwd_recv.at[i])
        for mm in range(GROUP):
            at = 2 * (first + mm)
            lhs[mm * 8 : mm * 8 + 8] = (
                ext[pl.ds(at, 8, stride=0), :] * (1.0 - eighth) + ext[pl.ds(at + 1, 8, stride=0), :] * eighth
            )
        high = lhs[...].astype(BF16)
        low = (lhs[...] - high.astype(F32)).astype(BF16)
        fbuf[...] = jnp.dot(jnp.concatenate([high, low], axis=1), ww[...], preferred_element_type=F32)

        def member(mm, total):
            fine = fbuf[rows_at(mm * 8, 8), :]
            return tuple(total[l] + fine * pert[first + mm, l].astype(F32) for l in range(LEVELS))

        total = lax.fori_loop(0, GROUP, member, tuple(ens[l] for l in range(LEVELS)), unroll=2)
        for l in range(LEVELS):
            ens[l] = total[l]
        return _

    def halves(n, _):
        return ensemble_group(n, _)

    lax.fori_loop(0, 4, halves, 0)

    lev_copies[0].wait_recv()
    lev_copies[1].wait_recv()
    to_rows(nat_s, v_s, lambda value: value)
    to_rows(nat_k, kap, jnp.sqrt)
    for copy in static_rows:
        copy.start()

    lax.fori_loop(4, 8, halves, 0)

    for copy in static_rows:
        copy.wait()
    loads[9].wait()
    kap[0:HALO] = jnp.where(w == 0, 0.0, kap[0:HALO])
    kap[11 * 64 : ALL_ROWS] = jnp.where(w == WIDE - 1, 0.0, kap[11 * 64 : ALL_ROWS])
    diffuse(v_s)
    to_natural(v_s, tmp)

    for i in (6, 7, 8):
        loads[i].wait()
    j = lax.broadcasted_iota(jnp.int32, (WIDE, 1024), 0)
    x = lax.broadcasted_iota(jnp.int32, (WIDE, 1024), 1)
    spread = jnp.where(x // 8 == j, 1.0, 0.0).astype(BF16)
    blocks = jnp.concatenate([jnp.where(hub[0:LEVELS] == 1, 1.0, 0.0), jnp.zeros((12, 128), F32)], axis=0).astype(BF16)
    hubx[...] = jnp.dot(blocks, spread, preferred_element_type=F32)
    for t in range(TILES):
        columns = slice(t * 128, t * 128 + 128)
        ocean = mask[t * 8 : t * 8 + 8].astype(F32)
        for l in range(LEVELS):
            at = (l * TILES + t) * 8
            there = rows_at(own0 + at, 8)
            inc = ocean * (SCALE * ens[l, :, columns] + tmp[there, :])
            incb[at : at + 8] = inc
            misfit = inc - inn[at : at + 8]
            is_huber = jnp.broadcast_to(hubx[l : l + 1, columns], (8, 128)) > 0.5
            weight = jnp.where(is_huber, 1.0 / jnp.maximum(jnp.abs(misfit), 1.0), 1.0)
            weighted = ocean * weight * misfit
            nat_w[there, :] = weighted
            wsc[l, :, columns] = weighted * SCALE
    lev_copies[2].start()
    inc_out = pltpu.make_async_copy(incb, inc_hbm, out_sem.at[0])
    inc_out.start()

    def adjoint_group(i, first_place):
        first = ((group + i) % GROUPS) * GROUP

        def member(mm, _):
            total = pert[first + mm, 0].astype(F32) * wsc[0]
            for l in range(1, LEVELS):
                total = total + pert[first + mm, l].astype(F32) * wsc[l]
            fbuf[rows_at(mm * 8, 8), :] = total
            return _

        lax.fori_loop(0, GROUP, member, 0, unroll=2)
        high = fbuf[...].astype(BF16)
        low = (fbuf[...] - high.astype(F32)).astype(BF16)
        gbuf[...] = jnp.dot(high, wt[...], preferred_element_type=F32) + jnp.dot(
            low, wt[...], preferred_element_type=F32
        )
        below = gbuf[pl.ds(0, GROUP, stride=8), :]
        above = jnp.zeros((GROUP, 128), F32)
        for r in range(1, 8):
            row = gbuf[pl.ds(r, GROUP, stride=8), :]
            below = below + row * (1.0 - r * 0.125)
            above = above + row * (r * 0.125)
        sb[pl.ds(2 * first, GROUP, stride=2), :] = below
        sb[pl.ds(2 * first + 1, GROUP, stride=2), :] = above

        def send(n, _):
            member_at = first + (place + n) % GROUP
            for k in range(2):
                remote(
                    sb.at[pl.ds(2 * member_at, 2)], bb.at[pl.ds(2 * (lev * WIDE + w), 2)], bwd_send, bwd_recv,
                    wide=member_at, level=(lev + 1 + k) % 2,
                ).start()
            return _

        lax.fori_loop(first_place, GROUP, send, 0)

    def adjoint_far(n, _):
        adjoint_group(offset_of(n), 0)
        return _

    lax.fori_loop(0, 5, adjoint_far, 0)

    lev_copies[2].wait_recv()
    to_rows(nat_w, v_w, lambda value: value)
    for copy in weighted_rows:
        copy.start()

    lax.fori_loop(5, 7, adjoint_far, 0)
    adjoint_group(0, 1)
    mine = pl.ds(2 * w, 2)
    slot = pl.ds(2 * (lev * WIDE + w), 2)
    remote(sb.at[mine], bb.at[slot], bwd_send, bwd_recv, level=1 - lev).start()
    pltpu.make_async_copy(sb.at[mine], bb.at[slot], bwd_recv).start()

    for copy in weighted_rows:
        copy.wait()
    diffuse(v_w)
    to_natural(v_w, tmp)
    sgb[...] = nat_s[pl.ds(own0, OWN), :] + tmp[pl.ds(own0, OWN), :]
    sg_out = pltpu.make_async_copy(sgb, sg_hbm, out_sem.at[1])
    sg_out.start()

    wait_bytes(bb, bwd_recv)
    terms = bb[0:256] + bb[256:512]
    rows_done = lax.dot_general(
        r2[...], terms, (((0,), (0,)), ((), ())), precision=PRECISE, preferred_element_type=F32
    )
    mgb[...] = mc[...] + lax.dot_general(
        rows_done, cf[...], (((1,), (1,)), ((), ())), precision=PRECISE, preferred_element_type=F32
    )
    mg_out = pltpu.make_async_copy(mgb, mg_hbm, out_sem.at[2])
    mg_out.start()

    wait_bytes(ext.at[pl.ds(0, 254)], fwd_send)
    wait_bytes(bb.at[pl.ds(0, 510)], bwd_send)
    for copy in lev_copies:
        copy.wait_send()
    inc_out.wait()
    sg_out.wait()
    mg_out.wait()


def natural(array):
    levels = array.shape[0]
    return array.reshape(levels, 8, TILES, 128).transpose(0, 2, 1, 3).reshape(levels * 64, 128)


def from_natural(array):
    return array.reshape(LEVELS, TILES, 8, 128).transpose(0, 2, 1, 3).reshape(LEVELS, 8, 1024)


def on_device(
    member_control, static_control, perturbations, innovation, diffusivity,
    rows_factor, column_factor, ocean_mask, huber_blocks, fold_map,
):
    hbm = pl.BlockSpec(memory_space=pltpu.HBM)
    dma = pltpu.SemaphoreType.DMA

    def vmem(*shape, dtype=F32):
        return pltpu.VMEM(shape, dtype)

    increment, member_gradient, static_gradient = pl.pallas_call(
        kernel,
        out_shape=(
            jax.ShapeDtypeStruct((OWN, 128), F32),
            jax.ShapeDtypeStruct((128, 128), F32),
            jax.ShapeDtypeStruct((OWN, 128), F32),
        ),
        in_specs=[hbm] * 10,
        out_specs=[hbm] * 3,
        scratch_shapes=[
            vmem(WIDE, LEVELS, 8, 1024, dtype=BF16),
            vmem(128, 128), vmem(128, 128), vmem(256, 128),
            vmem(256, 128), vmem(256, 128), vmem(512, 128), vmem(256, 128),
            vmem(512, 128), vmem(512, 128), vmem(512, 128),
            vmem(OWN, 128), vmem(64, 128, dtype=jnp.int32), vmem(8, 128, dtype=jnp.int32),
            vmem(8, 128, dtype=jnp.int32),
            vmem(ALL_ROWS, 128), vmem(ALL_ROWS, 128), vmem(ALL_ROWS, 128), vmem(ALL_ROWS, 128),
            vmem(512, 128),
            vmem(256, 1024, dtype=BF16), vmem(1024, 128, dtype=BF16),
            vmem(128, 128), vmem(128, 1024), vmem(128, 128),
            vmem(LEVELS, 8, 1024), vmem(LEVELS, 8, 1024), vmem(16, 1024),
            vmem(OWN, 128), vmem(OWN, 128), vmem(128, 128),
            dma((10,)), dma((3,)), dma, dma((8,)), dma, dma, dma((3,)), dma((3,)), dma((6,)), dma((6,)),
        ],
        compiler_params=pltpu.CompilerParams(
            collective_id=0, has_side_effects=True, vmem_limit_bytes=40 << 20
        ),
        name="increment_and_gradients",
    )(
        member_control.reshape(128, 128),
        natural(static_control),
        perturbations,
        natural(innovation),
        natural(diffusivity),
        rows_factor,
        column_factor,
        natural(ocean_mask[None]),
        huber_blocks.reshape(LEVELS, 128),
        fold_map.reshape(8, 128),
    )
    return from_natural(increment), member_gradient[None], from_natural(static_gradient)


def solution(mesh):
    return jax.shard_map(
        on_device,
        mesh=mesh,
        in_specs=(
            P("wide", None, None),
            P("lev", "wide", None),
            P(None, "lev", "wide", None),
            P("lev", "wide", None),
            P("lev", "wide", None),
            P(),
            P(),
            P("wide", None),
            P("lev", "wide", None),
            P(),
        ),
        out_specs=(P("lev", "wide", None), P("wide", None, None), P("lev", "wide", None)),
        check_vma=False,
    )
```

time: 175 us -> 66.4 us (0.38)
  the two profiles are of different devices: /device:TPU:24 before, /device:TPU:8 now
where the time goes in v1:
time: 66.4 us; the launch traced here: 66 us
  Pallas kernels  52.7 us (79%)
  local copies, waits for them, and re-layouts  12.7 us (19%)
    pallas_call x1, Pallas kernels, on_device(): pl.pallas_call(kernel, out_shape=(jax.ShapeDtypeStruct((OWN, 128), F32),...  52.7 us
    unnamed x23, local copies, waits for them, and re-layouts  12.7 us

profile of v1, /device:TPU:8, one launch (start us, length us, event | category | flops | bytes accessed | tf_op | source)
XLA Modules:
  0.0 66.0 jit_solution(8743508252005376359)
XLA Ops:
  0.6 0.0 copy-start
  0.6 3.4 %copy-done = bf16[128,4,8,1024]{3,2,1,0:T(8,128)(2,1)S(1)} copy-done((bf16[128,4,8,1024]{3,2,1,0:T(8,128)(2,1)S(1)}, bf16[128,4,8,1024]{3,2,1,0:T(8,128)(2,1)}, u32[]{:S(2)}) %copy-start) | copy-done | bytes 8388632
  4.0 0.0 copy-start.1
  4.0 0.9 %copy-done.1 = f32[4,8,1024]{2,1,0:T(8,128)S(1)} copy-done((f32[4,8,1024]{2,1,0:T(8,128)S(1)}, f32[4,8,1024]{2,1,0:T(8,128)}, u32[]{:S(2)}) %copy-start.1) | copy-done | bytes 131096
  4.9 0.0 copy-start.2
  4.9 0.9 %copy-done.2 = f32[4,8,1024]{2,1,0:T(8,128)S(1)} copy-done((f32[4,8,1024]{2,1,0:T(8,128)S(1)}, f32[4,8,1024]{2,1,0:T(8,128)}, u32[]{:S(2)}) %copy-start.2) | copy-done | bytes 131096
  5.8 0.0 copy-start.3
  5.8 0.9 %copy-done.3 = f32[4,8,1024]{2,1,0:T(8,128)S(1)} copy-done((f32[4,8,1024]{2,1,0:T(8,128)S(1)}, f32[4,8,1024]{2,1,0:T(8,128)}, u32[]{:S(2)}) %copy-start.3) | copy-done | bytes 131096
  6.7 0.0 copy-start.4
  6.7 0.8 %copy-done.4 = f32[1,128,128]{2,1,0:T(8,128)S(1)} copy-done((f32[1,128,128]{2,1,0:T(8,128)S(1)}, f32[1,128,128]{2,1,0:T(8,128)}, u32[]{:S(2)}) %copy-start.4) | copy-done | bytes 65560
  7.6 0.0 copy-start.5
  7.6 0.8 %copy-done.5 = f32[128,128]{1,0:T(8,128)S(1)} copy-done((f32[128,128]{1,0:T(8,128)S(1)}, f32[128,128]{1,0:T(8,128)}, u32[]{:S(2)}) %copy-start.5) | copy-done | bytes 65560
  8.4 0.0 copy-start.6
  8.4 0.8 %copy-done.6 = f32[128,128]{1,0:T(8,128)S(1)} copy-done((f32[128,128]{1,0:T(8,128)S(1)}, f32[128,128]{1,0:T(8,128)}, u32[]{:S(2)}) %copy-start.6) | copy-done | bytes 65560
  9.3 0.0 copy-start.7
  9.3 0.8 %copy-done.7 = s32[8,1024]{1,0:T(8,128)S(1)} copy-done((s32[8,1024]{1,0:T(8,128)S(1)}, s32[8,1024]{1,0:T(8,128)}, u32[]{:S(2)}) %copy-start.7) | copy-done | bytes 32792
  10.0 0.0 copy-start.8
  10.0 0.7 %copy-done.8 = s32[1024]{0:T(1024)S(1)} copy-done((s32[1024]{0:T(1024)S(1)}, s32[1024]{0:T(1024)}, u32[]{:S(2)}) %copy-start.8) | copy-done | bytes 4120
  10.7 0.0 copy-start.9
  10.7 0.7 %copy-done.9 = s32[4,1,128]{2,1,0:T(1,128)S(1)} copy-done((s32[4,1,128]{2,1,0:T(1,128)S(1)}, s32[4,1,128]{2,1,0:T(1,128)}, u32[]{:S(2)}) %copy-start.9) | copy-done | bytes 2072
  11.4 52.7 %increment_and_gradients.1 = (f32[256,128]{1,0:T(8,128)S(1)}, f32[128,128]{1,0:T(8,128)S(1)}, f32[256,128]{1,0:T(8,128)S(1)}) custom-call(f32[128,128]{1,0:T(8,128)S(1)} %bitcast.39, f32[256,128]{1,0:T(8,128)S(1)} %bitcast.34, bf16[128,4,8,1024]{3,2,1,0:T(8,128)(2,1)S(1)} %copy-done, f32[256,128]{1,0:T(8,128)S(1)} %bitcast.35, f32[256,128]{1,0:T(8,128)S(1)} %bitcast.36, ...), custom_call_target="tpu_custom_call" | custom-call | tf_op jit(solution)/shard_map/increment_and_gradients/pallas_call | solution.py:362
  64.0 0.7 copy.16
  64.7 0.6 copy.17
  65.3 0.7 copy.18
Async XLA Ops:
  0.6 3.4 %copy-start = (bf16[128,4,8,1024]{3,2,1,0:T(8,128)(2,1)S(1)}, bf16[128,4,8,1024]{3,2,1,0:T(8,128)(2,1)}, u32[]{:S(2)}) copy-start(bf16[128,4,8,1024]{3,2,1,0:T(8,128)(2,1)} %pert_hbm.1) | copy-start | bytes 25165828
  4.0 0.9 %copy-start.1 = (f32[4,8,1024]{2,1,0:T(8,128)S(1)}, f32[4,8,1024]{2,1,0:T(8,128)}, u32[]{:S(2)}) copy-start(f32[4,8,1024]{2,1,0:T(8,128)} %param.11) | copy-start | bytes 393220
  4.9 0.9 %copy-start.2 = (f32[4,8,1024]{2,1,0:T(8,128)S(1)}, f32[4,8,1024]{2,1,0:T(8,128)}, u32[]{:S(2)}) copy-start(f32[4,8,1024]{2,1,0:T(8,128)} %param.13) | copy-start | bytes 393220
  5.8 0.9 %copy-start.3 = (f32[4,8,1024]{2,1,0:T(8,128)S(1)}, f32[4,8,1024]{2,1,0:T(8,128)}, u32[]{:S(2)}) copy-start(f32[4,8,1024]{2,1,0:T(8,128)} %param.14) | copy-start | bytes 393220
  6.7 0.8 %copy-start.4 = (f32[1,128,128]{2,1,0:T(8,128)S(1)}, f32[1,128,128]{2,1,0:T(8,128)}, u32[]{:S(2)}) copy-start(f32[1,128,128]{2,1,0:T(8,128)} %param.10) | copy-start | bytes 196612
  7.6 0.8 %copy-start.5 = (f32[128,128]{1,0:T(8,128)S(1)}, f32[128,128]{1,0:T(8,128)}, u32[]{:S(2)}) copy-start(f32[128,128]{1,0:T(8,128)} %rf_hbm.1) | copy-start | bytes 196612
  8.4 0.8 %copy-start.6 = (f32[128,128]{1,0:T(8,128)S(1)}, f32[128,128]{1,0:T(8,128)}, u32[]{:S(2)}) copy-start(f32[128,128]{1,0:T(8,128)} %cf_hbm.1) | copy-start | bytes 196612
  9.3 0.8 %copy-start.7 = (s32[8,1024]{1,0:T(8,128)S(1)}, s32[8,1024]{1,0:T(8,128)}, u32[]{:S(2)}) copy-start(s32[8,1024]{1,0:T(8,128)} %param.17) | copy-start | bytes 98308
  10.0 0.7 %copy-start.8 = (s32[1024]{0:T(1024)S(1)}, s32[1024]{0:T(1024)}, u32[]{:S(2)}) copy-start(s32[1024]{0:T(1024)} %param.19) | copy-start | bytes 12292
  10.7 0.7 %copy-start.9 = (s32[4,1,128]{2,1,0:T(1,128)S(1)}, s32[4,1,128]{2,1,0:T(1,128)}, u32[]{:S(2)}) copy-start(s32[4,1,128]{2,1,0:T(1,128)} %param.18) | copy-start | bytes 6148

commit v2 on v1

--- a/solution.py
+++ b/solution.py
@@ -11,6 +11,8 @@
 WIDE = 128
 GROUP = 16
 GROUPS = WIDE // GROUP
+D_FIRST = True
+BEFORE = 5
 LEVELS = 4
 TILES = 8
 F32 = jnp.float32
@@ -21,6 +23,8 @@
 OWN = LEVELS * 64
 HALO = STEPS * 64
 ALL_ROWS = (8 + 2 * STEPS) * 64
+DOWN_SIZE = STEPS * LEVELS * 8
+PACKED = 2 * DOWN_SIZE + 48
 
 
 def rows_at(start, size, step=1):
@@ -33,8 +37,9 @@
     mc_hbm, sc_hbm, pert_hbm, inn_hbm, dif_hbm, rf_hbm, cf_hbm, mask_hbm, hub_hbm, fold_hbm,
     inc_hbm, mg_hbm, sg_hbm,
     pert, mc, cf, r2, win, ext, bb, sb, nat_s, nat_k, nat_w, inn, mask, hub, fold,
-    v_s, v_w, kap, s_buf, tmp, ww, wt, lhs, fbuf, gbuf, ens, wsc, hubx, incb, sgb, mgb,
-    load_sem, out_sem, fwd_send, fwd_recv, bwd_send, bwd_recv, lev_send, lev_recv, row_send, row_recv,
+    v_s, v_w, kap, s_a, s_b, tmp, ww, wt, lhs, fbuf, gbuf, ens, wsc, hubx, incb, sgb, mgb,
+    pack, pack_w, from_rows, from_rows_w, half, twin, table,
+    load_sem, out_sem, fwd_send, fwd_recv, bwd_send, bwd_recv, lev_send, lev_recv, row_send, row_recv, half_send, half_recv,
 ):
     w = lax.axis_index("wide")
     lev = lax.axis_index("lev")
@@ -50,15 +55,6 @@
 
     def wait_bytes(ref, sem):
         pltpu.make_async_copy(ref, ref, sem).wait()
-
-    barrier = pltpu.get_barrier_semaphore()
-
-    def tell(i, _):
-        pl.semaphore_signal(barrier, inc=1, device_id={"wide": (w + i) % WIDE, "lev": lev}, device_id_type=MESH)
-        return _
-
-    lax.fori_loop(1, WIDE, tell, 0)
-    pl.semaphore_signal(barrier, inc=1, device_id={"wide": w, "lev": 1 - lev}, device_id_type=MESH)
 
     loads = [
         (mc_hbm, mc), (cf_hbm, cf), (rf_hbm, tmp.at[pl.ds(0, 128)]),
@@ -69,17 +65,34 @@
     for load in loads:
         load.start()
 
-    j = lax.broadcasted_iota(jnp.int32, (WIDE, 1024), 0)
-    x = lax.broadcasted_iota(jnp.int32, (WIDE, 1024), 1)
-    part = (x % 8).astype(F32) * 0.125
-    weights = jnp.where(x // 8 == j, 1.0 - part, 0.0) + jnp.where((x // 8 + 1) % WIDE == j, part, 0.0)
-    ww[0:128] = weights.astype(BF16)
-    ww[128:256] = weights.astype(BF16)
-    x = lax.broadcasted_iota(jnp.int32, (1024, WIDE), 0)
-    j = lax.broadcasted_iota(jnp.int32, (1024, WIDE), 1)
-    part = (x % 8).astype(F32) * 0.125
-    weights = jnp.where(x // 8 == j, 1.0 - part, 0.0) + jnp.where((x // 8 + 1) % WIDE == j, part, 0.0)
-    wt[...] = weights.astype(BF16)
+    barrier = pltpu.get_barrier_semaphore()
+
+    def signal(wide, level):
+        pl.semaphore_signal(barrier, inc=1, device_id={"wide": wide, "lev": level}, device_id_type=MESH)
+
+    for wide in (w, left, right):
+        signal(wide, 1 - lev)
+
+    column = lax.broadcasted_iota(jnp.int32, (8, 1024), 1)
+    cell, part = column // 8, (column % 8).astype(F32) * 0.125
+
+    def table_and_signals(n, _):
+        j = lax.broadcasted_iota(jnp.int32, (8, 1024), 0) + n * 8
+        both = jnp.where(cell == j, 1.0 - part, 0.0) + jnp.where((cell + 1) % WIDE == j, part, 0.0)
+        table[rows_at(n * 8, 8), :] = both
+        for k in range(8):
+            signal((w + n * 8 + k + 1) % WIDE, lev)
+        return _
+
+    lax.fori_loop(0, 15, table_and_signals, 0)
+    j = lax.broadcasted_iota(jnp.int32, (8, 1024), 0) + 120
+    table[120:128] = jnp.where(cell == j, 1.0 - part, 0.0) + jnp.where((cell + 1) % WIDE == j, part, 0.0)
+    for k in range(7):
+        signal((w + 121 + k) % WIDE, lev)
+    weights = table[...].astype(BF16)
+    ww[0:128] = weights
+    ww[128:256] = weights
+    wt[...] = table[...].T.astype(BF16)
 
     for i in range(3):
         loads[i].wait()
@@ -88,33 +101,82 @@
     columns_done = jnp.dot(mc[...], cf[...], precision=PRECISE, preferred_element_type=F32)
     win[...] = jnp.dot(r2[...], columns_done, precision=PRECISE, preferred_element_type=F32)
 
-    pl.semaphore_wait(barrier, WIDE)
-
-    def offset_of(n):
-        return 4 + (1 - 2 * (n % 2)) * ((n + 1) // 2)
-
-    def send_window(n, _):
-        i = offset_of(n // GROUP)
-        to = ((group + i) % GROUPS) * GROUP + (place + n % GROUP) % GROUP
-        remote(win.at[pl.ds(2 * to, 2)], ext.at[pl.ds(2 * w, 2)], fwd_send, fwd_recv.at[i], wide=to).start()
-        return _
-
-    lax.fori_loop(0, 7 * GROUP, send_window, 0)
-    lax.fori_loop(7 * GROUP + 1, 8 * GROUP, send_window, 0)
-    pltpu.make_async_copy(win.at[pl.ds(2 * w, 2)], ext.at[pl.ds(2 * w, 2)], fwd_recv.at[0]).start()
-
-    for i in (3, 4):
-        loads[i].wait()
+    near, next_near = 3 * (1 - lev), 2 - lev
+
+    def pack_rows(nat, out, at):
+        def row(level, r):
+            return nat[pl.ds(own0 + level * 64 + r, 8, stride=8), :]
+
+        for k in range(STEPS):
+            for l in range(LEVELS):
+                out[pl.ds(at + (k * LEVELS + l) * 8, 8), :] = row(l, 5 + k)
+                out[pl.ds(at + DOWN_SIZE + (k * LEVELS + l) * 8, 8), :] = row(l, k)
+        for k, (level, r) in enumerate(((near, 7), (near, 6), (next_near, 7), (near, 0), (near, 1), (next_near, 0))):
+            out[pl.ds(at + 2 * DOWN_SIZE + k * 8, 8), :] = row(level, r)
+
+    def unpack_rows(got, at, out, change):
+        def put(r, level, value):
+            out[pl.ds(r * 64 + level, 8, stride=8), :] = change(value)
+
+        for k in range(STEPS):
+            for l in range(LEVELS):
+                put(k, lev * LEVELS + l, got[pl.ds(at + (k * LEVELS + l) * 8, 8), :])
+                put(11 + k, lev * LEVELS + l, got[pl.ds(at + DOWN_SIZE + (k * LEVELS + l) * 8, 8), :])
+        theirs, theirs_next = 4 - lev, 5 - 3 * lev
+        for k, (r, level) in enumerate(
+            ((2, theirs), (1, theirs), (2, theirs_next), (11, theirs), (12, theirs), (11, theirs_next))
+        ):
+            put(r, level, got[pl.ds(at + 2 * DOWN_SIZE + k * 8, 8), :])
+
+    def row_copies(out, got, at, i):
+        parts = (
+            (right, lev, 0, DOWN_SIZE), (left, lev, DOWN_SIZE, DOWN_SIZE),
+            (right, 1 - lev, 2 * DOWN_SIZE, 24), (left, 1 - lev, 2 * DOWN_SIZE + 24, 24),
+        )
+        return [
+            remote(
+                out.at[pl.ds(at + start, size)], got.at[pl.ds(at + start, size)],
+                row_send.at[i + k], row_recv.at[i + k], wide=wide, level=level,
+            )
+            for k, (wide, level, start, size) in enumerate(parts)
+        ]
+
     seen = pl.ds(pl.multiple_of(64 + 192 * lev, 64), 192)
     unseen = pl.ds(pl.multiple_of(448 * (1 - lev), 64), 64)
     lev_copies = [
         remote(nat.at[seen], nat.at[seen], lev_send.at[i], lev_recv.at[i], level=1 - lev)
         for i, nat in enumerate((nat_s, nat_k, nat_w))
     ]
+    static_rows = row_copies(pack, from_rows, 0, 0) + row_copies(pack, from_rows, PACKED, 4)
+    weighted_rows = row_copies(pack_w, from_rows_w, 0, 8)
+    for i in (3, 4):
+        loads[i].wait()
+    pack_rows(nat_s, pack, 0)
+    pack_rows(nat_k, pack, PACKED)
+    for nat in (nat_s, nat_k, nat_w):
+        nat[unseen, :] = jnp.zeros((64, 128), F32)
+    for rows in (v_s, v_w, kap):
+        rows[0:HALO] = jnp.zeros((HALO, 128), F32)
+        rows[11 * 64 : ALL_ROWS] = jnp.zeros((HALO, 128), F32)
+
+    pl.semaphore_wait(barrier, WIDE + 2)
     lev_copies[0].start()
     lev_copies[1].start()
-    for nat in (nat_s, nat_k, nat_w):
-        nat[unseen, :] = jnp.zeros((64, 128), F32)
+    for copy in static_rows:
+        copy.start()
+
+    def offset_of(n):
+        return 4 + (1 - 2 * (n % 2)) * ((n + 1) // 2)
+
+    def send_window(n, _):
+        i = offset_of(n // GROUP)
+        to = ((group + i) % GROUPS) * GROUP + (place + n % GROUP) % GROUP
+        remote(win.at[pl.ds(2 * to, 2)], ext.at[pl.ds(2 * w, 2)], fwd_send, fwd_recv.at[i], wide=to).start()
+        return _
+
+    lax.fori_loop(0, 7 * GROUP, send_window, 0)
+    lax.fori_loop(7 * GROUP + 1, 8 * GROUP, send_window, 0)
+    pltpu.make_async_copy(win.at[pl.ds(2 * w, 2)], ext.at[pl.ds(2 * w, 2)], fwd_recv.at[0]).start()
 
     def to_rows(nat, out, change):
         def body(r, _):
@@ -132,42 +194,33 @@
 
         lax.fori_loop(0, 8, body, 0)
 
-    def row_copies(rows, i):
-        down = remote(rows.at[pl.ds(8 * 64, HALO)], rows.at[pl.ds(0, HALO)], row_send.at[i], row_recv.at[i], wide=right)
-        up = remote(
-            rows.at[pl.ds(3 * 64, HALO)], rows.at[pl.ds(11 * 64, HALO)], row_send.at[i + 1], row_recv.at[i + 1], wide=left
-        )
-        return [down, up]
-
-    static_rows = row_copies(v_s, 0) + row_copies(kap, 2)
-    weighted_rows = row_copies(v_w, 4)
-
     sublane = lax.broadcasted_iota(jnp.int32, (8, 8, 128), 1)
     lane = lax.broadcasted_iota(jnp.int32, (64, 128), 1)
 
-    def fold_row(row):
+    def fold_row(s_buf):
         def body(t, _):
             entry = jnp.broadcast_to(fold[pl.ds(t, 1), :], (8, 128))
             at, tile = entry % 128, entry // 128
             total = jnp.zeros((8, 128), F32)
             for u in range(TILES):
-                there = jnp.take_along_axis(s_buf[pl.ds(row * 64 + u * 8, 8), :], at, axis=1)
+                there = jnp.take_along_axis(s_buf[pl.ds(10 * 64 + u * 8, 8), :], at, axis=1)
                 total = jnp.where(tile == u, there, total)
-            here = rows_at((row + 1) * 64 + t * 8, 8)
+            here = rows_at(11 * 64 + t * 8, 8)
             s_buf[here, :] = jnp.where(w == WIDE - 1, total, s_buf[here, :])
             return _
 
         lax.fori_loop(0, TILES, body, 0)
 
     def diffuse(v):
+        def scale_row(i, _):
+            here = rows_at(i * 64, 64)
+            s_a[here, :] = kap[here, :] * v[here, :]
+            return _
+
+        lax.fori_loop(0, 14, scale_row, 0, unroll=2)
         for step in range(1, STEPS + 1):
-            def scale_row(i, _):
-                here = rows_at(i * 64, 64)
-                s_buf[here, :] = kap[here, :] * v[here, :]
-                return _
-
-            lax.fori_loop(step - 1, 8 + 2 * STEPS + 1 - step, scale_row, 0)
-            fold_row(STEPS + 7)
+            s_buf, s_next = (s_a, s_b) if step % 2 else (s_b, s_a)
+            fold_row(s_buf)
 
             def update_row(i, _):
                 here = rows_at(i * 64, 64)
@@ -180,10 +233,13 @@
                 below = jnp.where(sublane == 0, 0.0, pltpu.roll(s3, 1, 1)).reshape(64, 128)
                 above = jnp.where(sublane == 7, 0.0, pltpu.roll(s3, 7, 1)).reshape(64, 128)
                 across = s_buf[rows_at(i * 64 + 64, 64), :] + s_buf[rows_at(i * 64 - 64, 64), :] + west + east
-                v[here, :] = v[here, :] + kap[here, :] * (across + 0.5 * (below + above) - 5.0 * s)
+                new = v[here, :] + kap[here, :] * (across + 0.5 * (below + above) - 5.0 * s)
+                v[here, :] = new
+                if step < STEPS:
+                    s_next[here, :] = kap[here, :] * new
                 return _
 
-            lax.fori_loop(step, 8 + 2 * STEPS - step, update_row, 0)
+            lax.fori_loop(step, 14 - step, update_row, 0, unroll=2)
 
     eighth = lax.broadcasted_iota(jnp.int32, (8, 128), 0).astype(F32) * 0.125
     loads[5].wait()
@@ -211,27 +267,20 @@
             ens[l] = total[l]
         return _
 
-    def halves(n, _):
-        return ensemble_group(n, _)
-
-    lax.fori_loop(0, 4, halves, 0)
-
-    lev_copies[0].wait_recv()
-    lev_copies[1].wait_recv()
+    lax.fori_loop(0, BEFORE, ensemble_group, 0)
+
+    for copy in lev_copies[:2] + static_rows:
+        copy.wait_recv()
     to_rows(nat_s, v_s, lambda value: value)
     to_rows(nat_k, kap, jnp.sqrt)
-    for copy in static_rows:
-        copy.start()
-
-    lax.fori_loop(4, 8, halves, 0)
-
-    for copy in static_rows:
-        copy.wait()
+    unpack_rows(from_rows, 0, v_s, lambda value: value)
+    unpack_rows(from_rows, PACKED, kap, jnp.sqrt)
     loads[9].wait()
     kap[0:HALO] = jnp.where(w == 0, 0.0, kap[0:HALO])
     kap[11 * 64 : ALL_ROWS] = jnp.where(w == WIDE - 1, 0.0, kap[11 * 64 : ALL_ROWS])
     diffuse(v_s)
     to_natural(v_s, tmp)
+    lax.fori_loop(BEFORE, 8, ensemble_group, 0)
 
     for i in (6, 7, 8):
         loads[i].wait()
@@ -255,6 +304,9 @@
             nat_w[there, :] = weighted
             wsc[l, :, columns] = weighted * SCALE
     lev_copies[2].start()
+    pack_rows(nat_w, pack_w, 0)
+    for copy in weighted_rows:
+        copy.start()
     inc_out = pltpu.make_async_copy(incb, inc_hbm, out_sem.at[0])
     inc_out.start()
 
@@ -285,11 +337,9 @@
 
         def send(n, _):
             member_at = first + (place + n) % GROUP
-            for k in range(2):
-                remote(
-                    sb.at[pl.ds(2 * member_at, 2)], bb.at[pl.ds(2 * (lev * WIDE + w), 2)], bwd_send, bwd_recv,
-                    wide=member_at, level=(lev + 1 + k) % 2,
-                ).start()
+            remote(
+                sb.at[pl.ds(2 * member_at, 2)], bb.at[pl.ds(2 * w, 2)], bwd_send, bwd_recv, wide=member_at
+            ).start()
             return _
 
         lax.fori_loop(first_place, GROUP, send, 0)
@@ -298,46 +348,64 @@
         adjoint_group(offset_of(n), 0)
         return _
 
-    lax.fori_loop(0, 5, adjoint_far, 0)
-
-    lev_copies[2].wait_recv()
-    to_rows(nat_w, v_w, lambda value: value)
-    for copy in weighted_rows:
-        copy.start()
-
-    lax.fori_loop(5, 7, adjoint_far, 0)
+    lax.fori_loop(0, 7, adjoint_far, 0)
     adjoint_group(0, 1)
     mine = pl.ds(2 * w, 2)
-    slot = pl.ds(2 * (lev * WIDE + w), 2)
-    remote(sb.at[mine], bb.at[slot], bwd_send, bwd_recv, level=1 - lev).start()
-    pltpu.make_async_copy(sb.at[mine], bb.at[slot], bwd_recv).start()
-
-    for copy in weighted_rows:
-        copy.wait()
-    diffuse(v_w)
-    to_natural(v_w, tmp)
-    sgb[...] = nat_s[pl.ds(own0, OWN), :] + tmp[pl.ds(own0, OWN), :]
+    pltpu.make_async_copy(sb.at[mine], bb.at[mine], bwd_recv).start()
+
+    def weighted_diffusion():
+        for copy in [lev_copies[2]] + weighted_rows:
+            copy.wait_recv()
+        to_rows(nat_w, v_w, lambda value: value)
+        unpack_rows(from_rows_w, 0, v_w, lambda value: value)
+        diffuse(v_w)
+        to_natural(v_w, tmp)
+        sgb[...] = nat_s[pl.ds(own0, OWN), :] + tmp[pl.ds(own0, OWN), :]
+
+    def half_gradient():
+        wait_bytes(bb, bwd_recv)
+        half[...] = lax.dot_general(
+            r2[...], bb[...], (((0,), (0,)), ((), ())), precision=PRECISE, preferred_element_type=F32
+        )
+        half_copy.start()
+
+    half_copy = remote(half, twin, half_send, half_recv, level=1 - lev)
+    if D_FIRST:
+        weighted_diffusion()
+        half_gradient()
+    else:
+        half_gradient()
+        weighted_diffusion()
     sg_out = pltpu.make_async_copy(sgb, sg_hbm, out_sem.at[1])
     sg_out.start()
 
-    wait_bytes(bb, bwd_recv)
-    terms = bb[0:256] + bb[256:512]
-    rows_done = lax.dot_general(
-        r2[...], terms, (((0,), (0,)), ((), ())), precision=PRECISE, preferred_element_type=F32
-    )
+    half_copy.wait_recv()
     mgb[...] = mc[...] + lax.dot_general(
-        rows_done, cf[...], (((1,), (1,)), ((), ())), precision=PRECISE, preferred_element_type=F32
+        half[...] + twin[...], cf[...], (((1,), (1,)), ((), ())), precision=PRECISE, preferred_element_type=F32
     )
     mg_out = pltpu.make_async_copy(mgb, mg_hbm, out_sem.at[2])
     mg_out.start()
 
     wait_bytes(ext.at[pl.ds(0, 254)], fwd_send)
-    wait_bytes(bb.at[pl.ds(0, 510)], bwd_send)
-    for copy in lev_copies:
+    wait_bytes(ext.at[pl.ds(0, 254)], bwd_send)
+    for copy in lev_copies + static_rows + weighted_rows + [half_copy]:
         copy.wait_send()
     inc_out.wait()
     sg_out.wait()
     mg_out.wait()
+
+
+def finish(*refs):
+    sources, results, held, sem = refs[:3], refs[3:6], refs[6:9], refs[9]
+    inward = [pltpu.make_async_copy(a, b, sem.at[0, i]) for i, (a, b) in enumerate(zip(sources, held))]
+    outward = [pltpu.make_async_copy(a, b, sem.at[1, i]) for i, (a, b) in enumerate(zip(held, results))]
+    for copy in inward:
+        copy.start()
+    for into, out in zip(inward, outward):
+        into.wait()
+        out.start()
+    for copy in outward:
+        copy.wait()
 
 
 def natural(array):
@@ -371,20 +439,23 @@
         scratch_shapes=[
             vmem(WIDE, LEVELS, 8, 1024, dtype=BF16),
             vmem(128, 128), vmem(128, 128), vmem(256, 128),
-            vmem(256, 128), vmem(256, 128), vmem(512, 128), vmem(256, 128),
+            vmem(256, 128), vmem(256, 128), vmem(256, 128), vmem(256, 128),
             vmem(512, 128), vmem(512, 128), vmem(512, 128),
             vmem(OWN, 128), vmem(64, 128, dtype=jnp.int32), vmem(8, 128, dtype=jnp.int32),
             vmem(8, 128, dtype=jnp.int32),
-            vmem(ALL_ROWS, 128), vmem(ALL_ROWS, 128), vmem(ALL_ROWS, 128), vmem(ALL_ROWS, 128),
+            vmem(ALL_ROWS, 128), vmem(ALL_ROWS, 128), vmem(ALL_ROWS, 128),
+            vmem(ALL_ROWS, 128), vmem(ALL_ROWS, 128),
             vmem(512, 128),
             vmem(256, 1024, dtype=BF16), vmem(1024, 128, dtype=BF16),
             vmem(128, 128), vmem(128, 1024), vmem(128, 128),
             vmem(LEVELS, 8, 1024), vmem(LEVELS, 8, 1024), vmem(16, 1024),
             vmem(OWN, 128), vmem(OWN, 128), vmem(128, 128),
-            dma((10,)), dma((3,)), dma, dma((8,)), dma, dma, dma((3,)), dma((3,)), dma((6,)), dma((6,)),
+            vmem(2 * PACKED, 128), vmem(PACKED, 128), vmem(2 * PACKED, 128), vmem(PACKED, 128),
+            vmem(128, 128), vmem(128, 128), vmem(WIDE, 1024),
+            dma((10,)), dma((3,)), dma, dma((8,)), dma, dma, dma((3,)), dma((3,)), dma((12,)), dma((12,)), dma, dma,
         ],
         compiler_params=pltpu.CompilerParams(
-            collective_id=0, has_side_effects=True, vmem_limit_bytes=40 << 20
+            collective_id=0, has_side_effects=True, vmem_limit_bytes=63 << 20
         ),
         name="increment_and_gradients",
     )(
@@ -399,6 +470,19 @@
         huber_blocks.reshape(LEVELS, 128),
         fold_map.reshape(8, 128),
     )
+    increment, member_gradient, static_gradient = pl.pallas_call(
+        finish,
+        out_shape=(
+            jax.ShapeDtypeStruct((OWN, 128), F32),
+            jax.ShapeDtypeStruct((128, 128), F32),
+            jax.ShapeDtypeStruct((OWN, 128), F32),
+        ),
+        in_specs=[hbm] * 3,
+        out_specs=[hbm] * 3,
+        scratch_shapes=[vmem(OWN, 128), vmem(128, 128), vmem(OWN, 128), dma((2, 3))],
+        compiler_params=pltpu.CompilerParams(vmem_limit_bytes=63 << 20),
+        name="finish",
+    )(increment, member_gradient, static_gradient)
     return from_natural(increment), member_gradient[None], from_natural(static_gradient)
 
 

time: 66.4 us -> 49.3 us (0.74)
  the two profiles are of different devices: /device:TPU:8 before, /device:TPU:1 now
where the time goes in v2:
time: 49.3 us; the launch traced here: 49.2 us
  Pallas kernels  48.6 us (99%)
  between operations  0.64 us (1%)
    pallas_call x1, Pallas kernels, on_device(): pl.pallas_call(kernel, out_shape=(jax.ShapeDtypeStruct((OWN, 128), F32),...  46.9 us
    pallas_call x1, Pallas kernels, on_device(): pl.pallas_call(finish, out_shape=(jax.ShapeDtypeStruct((OWN, 128), F32),...  1.71 us

profile of v2, /device:TPU:1, one launch (start us, length us, event | category | flops | bytes accessed | tf_op | source)
XLA Modules:
  0.0 49.2 jit_solution(8607237756229973470)
XLA Ops:
  0.6 46.9 %increment_and_gradients.1 = (f32[256,128]{1,0:T(8,128)}, f32[128,128]{1,0:T(8,128)}, f32[256,128]{1,0:T(8,128)}) custom-call(f32[128,128]{1,0:T(8,128)} %bitcast.37, f32[256,128]{1,0:T(8,128)} %bitcast.34, bf16[128,4,8,1024]{3,2,1,0:T(8,128)(2,1)} %pert_hbm.1, f32[256,128]{1,0:T(8,128)} %bitcast.35, f32[256,128]{1,0:T(8,128)} %bitcast.36, ...), custom_call_target="tpu_custom_call" | custom-call | tf_op jit(solution)/shard_map/increment_and_gradients/pallas_call | solution.py:430
  47.5 1.7 %finish.1 = (f32[256,128]{1,0:T(8,128)}, f32[128,128]{1,0:T(8,128)}, f32[256,128]{1,0:T(8,128)}) custom-call(f32[256,128]{1,0:T(8,128)} %get-tuple-element.9.refs_0_, f32[128,128]{1,0:T(8,128)} %get-tuple-element.10.refs_1_, f32[256,128]{1,0:T(8,128)} %get-tuple-element.11.refs_2_), custom_call_target="tpu_custom_call" | custom-call | tf_op jit(solution)/shard_map/finish/pallas_call | solution.py:473

commit v3 on v2

--- a/solution.py
+++ b/solution.py
@@ -11,8 +11,8 @@
 WIDE = 128
 GROUP = 16
 GROUPS = WIDE // GROUP
-D_FIRST = True
-BEFORE = 5
+D_FIRST = False
+BEFORE = 3
 LEVELS = 4
 TILES = 8
 F32 = jnp.float32
@@ -37,8 +37,8 @@
     mc_hbm, sc_hbm, pert_hbm, inn_hbm, dif_hbm, rf_hbm, cf_hbm, mask_hbm, hub_hbm, fold_hbm,
     inc_hbm, mg_hbm, sg_hbm,
     pert, mc, cf, r2, win, ext, bb, sb, nat_s, nat_k, nat_w, inn, mask, hub, fold,
-    v_s, v_w, kap, s_a, s_b, tmp, ww, wt, lhs, fbuf, gbuf, ens, wsc, hubx, incb, sgb, mgb,
-    pack, pack_w, from_rows, from_rows_w, half, twin, table,
+    v_s, v_w, kap, s_a, s_b, tmp, ww, wt, parts, fbuf, gbuf, ens, wsc, hubx, incb, sgb, mgb,
+    pack, pack_w, from_rows, from_rows_w, half, twin, table, bb_late,
     load_sem, out_sem, fwd_send, fwd_recv, bwd_send, bwd_recv, lev_send, lev_recv, row_send, row_recv, half_send, half_recv,
 ):
     w = lax.axis_index("wide")
@@ -165,17 +165,16 @@
     for copy in static_rows:
         copy.start()
 
-    def offset_of(n):
-        return 4 + (1 - 2 * (n % 2)) * ((n + 1) // 2)
+    def near_first(n):
+        return n + (n // 2) * (5 - 2 * n)
 
     def send_window(n, _):
-        i = offset_of(n // GROUP)
+        i = near_first(n // (2 * GROUP)) + 4 * (n // GROUP % 2)
         to = ((group + i) % GROUPS) * GROUP + (place + n % GROUP) % GROUP
         remote(win.at[pl.ds(2 * to, 2)], ext.at[pl.ds(2 * w, 2)], fwd_send, fwd_recv.at[i], wide=to).start()
         return _
 
-    lax.fori_loop(0, 7 * GROUP, send_window, 0)
-    lax.fori_loop(7 * GROUP + 1, 8 * GROUP, send_window, 0)
+    lax.fori_loop(1, WIDE, send_window, 0)
     pltpu.make_async_copy(win.at[pl.ds(2 * w, 2)], ext.at[pl.ds(2 * w, 2)], fwd_recv.at[0]).start()
 
     def to_rows(nat, out, change):
@@ -203,13 +202,16 @@
             at, tile = entry % 128, entry // 128
             total = jnp.zeros((8, 128), F32)
             for u in range(TILES):
-                there = jnp.take_along_axis(s_buf[pl.ds(10 * 64 + u * 8, 8), :], at, axis=1)
+                there = jnp.take_along_axis(
+                    s_buf[pl.ds(10 * 64 + u * 8, 8), :], at, axis=1, mode="promise_in_bounds"
+                )
                 total = jnp.where(tile == u, there, total)
-            here = rows_at(11 * 64 + t * 8, 8)
-            s_buf[here, :] = jnp.where(w == WIDE - 1, total, s_buf[here, :])
+            s_buf[rows_at(11 * 64 + t * 8, 8), :] = total
             return _
 
-        lax.fori_loop(0, TILES, body, 0)
+        @pl.when(w == WIDE - 1)
+        def _():
+            lax.fori_loop(0, TILES, body, 0, unroll=4)
 
     def diffuse(v):
         def scale_row(i, _):
@@ -239,35 +241,39 @@
                     s_next[here, :] = kap[here, :] * new
                 return _
 
-            lax.fori_loop(step, 14 - step, update_row, 0, unroll=2)
-
-    eighth = lax.broadcasted_iota(jnp.int32, (8, 128), 0).astype(F32) * 0.125
+            lax.fori_loop(step, 14 - step, update_row, 0, unroll=4)
+
+    eighth = lax.broadcasted_iota(jnp.int32, (8, 1024), 0).astype(F32) * 0.125
     loads[5].wait()
     ens[...] = jnp.zeros((LEVELS, 8, 1024), F32)
 
-    def ensemble_group(n, _):
-        i = offset_of(7 - n)
-        first = ((group + GROUPS - i) % GROUPS) * GROUP
-        wait_bytes(ext.at[pl.ds(0, 2 * GROUP)], fwd_recv.at[i])
-        for mm in range(GROUP):
-            at = 2 * (first + mm)
-            lhs[mm * 8 : mm * 8 + 8] = (
-                ext[pl.ds(at, 8, stride=0), :] * (1.0 - eighth) + ext[pl.ds(at + 1, 8, stride=0), :] * eighth
-            )
-        high = lhs[...].astype(BF16)
-        low = (lhs[...] - high.astype(F32)).astype(BF16)
-        fbuf[...] = jnp.dot(jnp.concatenate([high, low], axis=1), ww[...], preferred_element_type=F32)
-
-        def member(mm, total):
-            fine = fbuf[rows_at(mm * 8, 8), :]
-            return tuple(total[l] + fine * pert[first + mm, l].astype(F32) for l in range(LEVELS))
-
-        total = lax.fori_loop(0, GROUP, member, tuple(ens[l] for l in range(LEVELS)), unroll=2)
+    def ensemble_pair(n, _):
+        firsts = []
+        for i in (near_first(n), near_first(n) + 4):
+            wait_bytes(ext.at[pl.ds(0, 2 * GROUP)], fwd_recv.at[i])
+            firsts.append(((group + GROUPS - i) % GROUPS) * GROUP)
+        coarse = jnp.concatenate([ext[rows_at(2 * first, 2 * GROUP), :] for first in firsts], axis=0)
+        high = coarse.astype(BF16)
+        low = (coarse - high.astype(F32)).astype(BF16)
+        fbuf[0 : 4 * GROUP] = jnp.dot(
+            jnp.concatenate([high, low], axis=1), ww[...], preferred_element_type=F32
+        )
+        total = tuple(ens[l] for l in range(LEVELS))
+        for k, first in enumerate(firsts):
+
+            def member(mm, total):
+                at = 2 * GROUP * k + 2 * mm
+                row = jnp.broadcast_to(fbuf[pl.ds(at, 1), :], (8, 1024))
+                after = jnp.broadcast_to(fbuf[pl.ds(at + 1, 1), :], (8, 1024))
+                fine = row + (after - row) * eighth
+                return tuple(total[l] + fine * pert[first + mm, l].astype(F32) for l in range(LEVELS))
+
+            total = lax.fori_loop(0, GROUP, member, total, unroll=2)
         for l in range(LEVELS):
             ens[l] = total[l]
         return _
 
-    lax.fori_loop(0, BEFORE, ensemble_group, 0)
+    lax.fori_loop(0, BEFORE, ensemble_pair, 0)
 
     for copy in lev_copies[:2] + static_rows:
         copy.wait_recv()
@@ -280,7 +286,7 @@
     kap[11 * 64 : ALL_ROWS] = jnp.where(w == WIDE - 1, 0.0, kap[11 * 64 : ALL_ROWS])
     diffuse(v_s)
     to_natural(v_s, tmp)
-    lax.fori_loop(BEFORE, 8, ensemble_group, 0)
+    lax.fori_loop(BEFORE, 4, ensemble_pair, 0)
 
     for i in (6, 7, 8):
         loads[i].wait()
@@ -310,48 +316,58 @@
     inc_out = pltpu.make_async_copy(incb, inc_hbm, out_sem.at[0])
     inc_out.start()
 
-    def adjoint_group(i, first_place):
-        first = ((group + i) % GROUPS) * GROUP
-
-        def member(mm, _):
-            total = pert[first + mm, 0].astype(F32) * wsc[0]
-            for l in range(1, LEVELS):
-                total = total + pert[first + mm, l].astype(F32) * wsc[l]
-            fbuf[rows_at(mm * 8, 8), :] = total
-            return _
-
-        lax.fori_loop(0, GROUP, member, 0, unroll=2)
-        high = fbuf[...].astype(BF16)
-        low = (fbuf[...] - high.astype(F32)).astype(BF16)
-        gbuf[...] = jnp.dot(high, wt[...], preferred_element_type=F32) + jnp.dot(
-            low, wt[...], preferred_element_type=F32
-        )
-        below = gbuf[pl.ds(0, GROUP, stride=8), :]
-        above = jnp.zeros((GROUP, 128), F32)
+    def adjoint_pair(n, offsets, late):
+        firsts = [((group + i) % GROUPS) * GROUP for i in offsets]
+        for k, first in enumerate(firsts):
+
+            def member(mm, _):
+                total = pert[first + mm, 0].astype(F32) * wsc[0]
+                for l in range(1, LEVELS):
+                    total = total + pert[first + mm, l].astype(F32) * wsc[l]
+                fbuf[rows_at((GROUP * k + mm) * 8, 8), :] = total
+                return _
+
+            lax.fori_loop(0, GROUP, member, 0, unroll=2)
+        terms = fbuf[...]
+        high = terms.astype(BF16)
+        parts[0:256] = high
+        parts[256:512] = (terms - high.astype(F32)).astype(BF16)
+        columns_done = jnp.dot(parts[...], wt[...], preferred_element_type=F32)
+        gbuf[...] = columns_done[0:256] + columns_done[256:512]
+        below = gbuf[pl.ds(0, 2 * GROUP, stride=8), :]
+        above = jnp.zeros((2 * GROUP, 128), F32)
         for r in range(1, 8):
-            row = gbuf[pl.ds(r, GROUP, stride=8), :]
+            row = gbuf[pl.ds(r, 2 * GROUP, stride=8), :]
             below = below + row * (1.0 - r * 0.125)
             above = above + row * (r * 0.125)
-        sb[pl.ds(2 * first, GROUP, stride=2), :] = below
-        sb[pl.ds(2 * first + 1, GROUP, stride=2), :] = above
-
-        def send(n, _):
-            member_at = first + (place + n) % GROUP
-            remote(
-                sb.at[pl.ds(2 * member_at, 2)], bb.at[pl.ds(2 * w, 2)], bwd_send, bwd_recv, wide=member_at
-            ).start()
-            return _
-
-        lax.fori_loop(first_place, GROUP, send, 0)
+        for k, first in enumerate(firsts):
+            sb[pl.ds(2 * first, GROUP, stride=2), :] = below[k * GROUP : (k + 1) * GROUP]
+            sb[pl.ds(2 * first + 1, GROUP, stride=2), :] = above[k * GROUP : (k + 1) * GROUP]
+
+            def send(p, _):
+                member_at = first + (place + p) % GROUP
+                source = sb.at[pl.ds(2 * member_at, 2)]
+                if late:
+                    slot = bb_late.at[pl.ds(2 * (64 * lev + (2 * n - 4 + k) * GROUP + place), 2)]
+                    remote(source, slot, bwd_send, bwd_recv.at[1], wide=member_at, level=1 - lev).start()
+                else:
+                    slot = bb.at[pl.ds(2 * ((2 * n + k) * GROUP + place), 2)]
+                remote(source, slot, bwd_send, bwd_recv.at[1 if late else 0], wide=member_at).start()
+                return _
+
+            lax.fori_loop(1 if late and offsets[k] == 0 else 0, GROUP, send, 0)
 
     def adjoint_far(n, _):
-        adjoint_group(offset_of(n), 0)
+        adjoint_pair(n, (2 - n, 6 - n), False)
         return _
 
-    lax.fori_loop(0, 7, adjoint_far, 0)
-    adjoint_group(0, 1)
+    lax.fori_loop(0, 2, adjoint_far, 0)
+    adjoint_pair(2, (3, 7), True)
+    adjoint_pair(3, (4, 0), True)
     mine = pl.ds(2 * w, 2)
-    pltpu.make_async_copy(sb.at[mine], bb.at[mine], bwd_recv).start()
+    slot = pl.ds(2 * (64 * lev + 3 * GROUP + place), 2)
+    remote(sb.at[mine], bb_late.at[slot], bwd_send, bwd_recv.at[1], level=1 - lev).start()
+    pltpu.make_async_copy(sb.at[mine], bb_late.at[slot], bwd_recv.at[1]).start()
 
     def weighted_diffusion():
         for copy in [lev_copies[2]] + weighted_rows:
@@ -362,11 +378,16 @@
         to_natural(v_w, tmp)
         sgb[...] = nat_s[pl.ds(own0, OWN), :] + tmp[pl.ds(own0, OWN), :]
 
+    def rows_adjoint(terms, offsets):
+        blocks = [r2[rows_at(((group + GROUPS - i) % GROUPS) * 2 * GROUP, 2 * GROUP), :] for i in offsets]
+        return lax.dot_general(
+            jnp.concatenate(blocks, axis=0), terms, (((0,), (0,)), ((), ())),
+            precision=PRECISE, preferred_element_type=F32,
+        )
+
     def half_gradient():
-        wait_bytes(bb, bwd_recv)
-        half[...] = lax.dot_general(
-            r2[...], bb[...], (((0,), (0,)), ((), ())), precision=PRECISE, preferred_element_type=F32
-        )
+        wait_bytes(bb, bwd_recv.at[0])
+        half[...] = rows_adjoint(bb[...], (2, 6, 1, 5))
         half_copy.start()
 
     half_copy = remote(half, twin, half_send, half_recv, level=1 - lev)
@@ -379,15 +400,17 @@
     sg_out = pltpu.make_async_copy(sgb, sg_hbm, out_sem.at[1])
     sg_out.start()
 
+    wait_bytes(bb_late, bwd_recv.at[1])
+    rows_done = half[...] + rows_adjoint(bb_late[0:128] + bb_late[128:256], (3, 7, 4, 0))
     half_copy.wait_recv()
     mgb[...] = mc[...] + lax.dot_general(
-        half[...] + twin[...], cf[...], (((1,), (1,)), ((), ())), precision=PRECISE, preferred_element_type=F32
+        rows_done + twin[...], cf[...], (((1,), (1,)), ((), ())), precision=PRECISE, preferred_element_type=F32
     )
     mg_out = pltpu.make_async_copy(mgb, mg_hbm, out_sem.at[2])
     mg_out.start()
 
     wait_bytes(ext.at[pl.ds(0, 254)], fwd_send)
-    wait_bytes(ext.at[pl.ds(0, 254)], bwd_send)
+    wait_bytes(nat_s.at[pl.ds(0, 2 * 192 - 2)], bwd_send)
     for copy in lev_copies + static_rows + weighted_rows + [half_copy]:
         copy.wait_send()
     inc_out.wait()
@@ -439,7 +462,7 @@
         scratch_shapes=[
             vmem(WIDE, LEVELS, 8, 1024, dtype=BF16),
             vmem(128, 128), vmem(128, 128), vmem(256, 128),
-            vmem(256, 128), vmem(256, 128), vmem(256, 128), vmem(256, 128),
+            vmem(256, 128), vmem(256, 128), vmem(128, 128), vmem(256, 128),
             vmem(512, 128), vmem(512, 128), vmem(512, 128),
             vmem(OWN, 128), vmem(64, 128, dtype=jnp.int32), vmem(8, 128, dtype=jnp.int32),
             vmem(8, 128, dtype=jnp.int32),
@@ -447,12 +470,12 @@
             vmem(ALL_ROWS, 128), vmem(ALL_ROWS, 128),
             vmem(512, 128),
             vmem(256, 1024, dtype=BF16), vmem(1024, 128, dtype=BF16),
-            vmem(128, 128), vmem(128, 1024), vmem(128, 128),
+            vmem(512, 1024, dtype=BF16), vmem(256, 1024), vmem(256, 128),
             vmem(LEVELS, 8, 1024), vmem(LEVELS, 8, 1024), vmem(16, 1024),
             vmem(OWN, 128), vmem(OWN, 128), vmem(128, 128),
             vmem(2 * PACKED, 128), vmem(PACKED, 128), vmem(2 * PACKED, 128), vmem(PACKED, 128),
-            vmem(128, 128), vmem(128, 128), vmem(WIDE, 1024),
-            dma((10,)), dma((3,)), dma, dma((8,)), dma, dma, dma((3,)), dma((3,)), dma((12,)), dma((12,)), dma, dma,
+            vmem(128, 128), vmem(128, 128), vmem(WIDE, 1024), vmem(256, 128),
+            dma((10,)), dma((3,)), dma, dma((8,)), dma, dma((2,)), dma((3,)), dma((3,)), dma((12,)), dma((12,)), dma, dma,
         ],
         compiler_params=pltpu.CompilerParams(
             collective_id=0, has_side_effects=True, vmem_limit_bytes=63 << 20

time: 49.3 us -> 45 us (0.913)
  Pallas kernels: 48.6 us -> 44.2 us
    pallas_call x1, Pallas kernels: 46.9 us -> 42.5 us  [on_device(): pl.pallas_call(kernel, out_shape=(jax.ShapeDtypeStruct((OWN, 128), F32),...]
where the time goes in v3:
time: 45 us; the launch traced here: 44.9 us
  Pallas kernels  44.2 us (98%)
  between operations  0.64 us (1%)
    pallas_call x1, Pallas kernels, on_device(): pl.pallas_call(kernel, out_shape=(jax.ShapeDtypeStruct((OWN, 128), F32),...  42.5 us
    pallas_call x1, Pallas kernels, on_device(): pl.pallas_call(finish, out_shape=(jax.ShapeDtypeStruct((OWN, 128), F32),...  1.71 us

profile of v3, /device:TPU:1, one launch (start us, length us, event | category | flops | bytes accessed | tf_op | source)
XLA Modules:
  0.0 44.9 jit_solution(14857844291267656924)
XLA Ops:
  0.6 42.5 %increment_and_gradients.1 = (f32[256,128]{1,0:T(8,128)}, f32[128,128]{1,0:T(8,128)}, f32[256,128]{1,0:T(8,128)}) custom-call(f32[128,128]{1,0:T(8,128)} %bitcast.37, f32[256,128]{1,0:T(8,128)} %bitcast.34, bf16[128,4,8,1024]{3,2,1,0:T(8,128)(2,1)} %pert_hbm.1, f32[256,128]{1,0:T(8,128)} %bitcast.35, f32[256,128]{1,0:T(8,128)} %bitcast.36, ...), custom_call_target="tpu_custom_call" | custom-call | tf_op jit(solution)/shard_map/increment_and_gradients/pallas_call | solution.py:453
  43.2 1.7 %finish.1 = (f32[256,128]{1,0:T(8,128)}, f32[128,128]{1,0:T(8,128)}, f32[256,128]{1,0:T(8,128)}) custom-call(f32[256,128]{1,0:T(8,128)} %get-tuple-element.9.refs_0_, f32[128,128]{1,0:T(8,128)} %get-tuple-element.10.refs_1_, f32[256,128]{1,0:T(8,128)} %get-tuple-element.11.refs_2_), custom_call_target="tpu_custom_call" | custom-call | tf_op jit(solution)/shard_map/finish/pallas_call | solution.py:496

commit v4 on v3

--- a/solution.py
+++ b/solution.py
@@ -12,6 +12,9 @@
 GROUP = 16
 GROUPS = WIDE // GROUP
 D_FIRST = False
+EARLY = 2
+PAIRS = ((2, 6), (1, 7), (3, 5), (4, 0))
+LATE_TILES = (4 - EARLY) * 2 * GROUP
 BEFORE = 3
 LEVELS = 4
 TILES = 8
@@ -89,10 +92,6 @@
     table[120:128] = jnp.where(cell == j, 1.0 - part, 0.0) + jnp.where((cell + 1) % WIDE == j, part, 0.0)
     for k in range(7):
         signal((w + 121 + k) % WIDE, lev)
-    weights = table[...].astype(BF16)
-    ww[0:128] = weights
-    ww[128:256] = weights
-    wt[...] = table[...].T.astype(BF16)
 
     for i in range(3):
         loads[i].wait()
@@ -151,31 +150,40 @@
     weighted_rows = row_copies(pack_w, from_rows_w, 0, 8)
     for i in (3, 4):
         loads[i].wait()
+
+    pl.semaphore_wait(barrier, WIDE + 2)
+    lev_copies[0].start()
+    lev_copies[1].start()
+
+    def near_first(n):
+        a = n + (n // 2) * (5 - 2 * n)
+        return a, 8 - a - 4 * ((3 - n) // 3)
+
+    def send_window(n, _):
+        a, b = near_first((WIDE - 1 - n) // (2 * GROUP))
+        i = a + (b - a) * (n % 2)
+        to = ((group + i) % GROUPS) * GROUP + (place + (n // 2) % GROUP) % GROUP
+        remote(win.at[pl.ds(2 * to, 2)], ext.at[pl.ds(2 * w, 2)], fwd_send, fwd_recv.at[i], wide=to).start()
+        return _
+
+    own = WIDE - 2 * GROUP
+    lax.fori_loop(0, own, send_window, 0)
+    lax.fori_loop(own + 1, WIDE, send_window, 0)
+    pltpu.make_async_copy(win.at[pl.ds(2 * w, 2)], ext.at[pl.ds(2 * w, 2)], fwd_recv.at[0]).start()
+
     pack_rows(nat_s, pack, 0)
     pack_rows(nat_k, pack, PACKED)
+    for copy in static_rows:
+        copy.start()
+    weights = table[...].astype(BF16)
+    ww[0:128] = weights
+    ww[128:256] = weights
+    wt[...] = table[...].T.astype(BF16)
     for nat in (nat_s, nat_k, nat_w):
         nat[unseen, :] = jnp.zeros((64, 128), F32)
     for rows in (v_s, v_w, kap):
         rows[0:HALO] = jnp.zeros((HALO, 128), F32)
         rows[11 * 64 : ALL_ROWS] = jnp.zeros((HALO, 128), F32)
-
-    pl.semaphore_wait(barrier, WIDE + 2)
-    lev_copies[0].start()
-    lev_copies[1].start()
-    for copy in static_rows:
-        copy.start()
-
-    def near_first(n):
-        return n + (n // 2) * (5 - 2 * n)
-
-    def send_window(n, _):
-        i = near_first(n // (2 * GROUP)) + 4 * (n // GROUP % 2)
-        to = ((group + i) % GROUPS) * GROUP + (place + n % GROUP) % GROUP
-        remote(win.at[pl.ds(2 * to, 2)], ext.at[pl.ds(2 * w, 2)], fwd_send, fwd_recv.at[i], wide=to).start()
-        return _
-
-    lax.fori_loop(1, WIDE, send_window, 0)
-    pltpu.make_async_copy(win.at[pl.ds(2 * w, 2)], ext.at[pl.ds(2 * w, 2)], fwd_recv.at[0]).start()
 
     def to_rows(nat, out, change):
         def body(r, _):
@@ -249,7 +257,7 @@
 
     def ensemble_pair(n, _):
         firsts = []
-        for i in (near_first(n), near_first(n) + 4):
+        for i in near_first(n):
             wait_bytes(ext.at[pl.ds(0, 2 * GROUP)], fwd_recv.at[i])
             firsts.append(((group + GROUPS - i) % GROUPS) * GROUP)
         coarse = jnp.concatenate([ext[rows_at(2 * first, 2 * GROUP), :] for first in firsts], axis=0)
@@ -348,7 +356,7 @@
                 member_at = first + (place + p) % GROUP
                 source = sb.at[pl.ds(2 * member_at, 2)]
                 if late:
-                    slot = bb_late.at[pl.ds(2 * (64 * lev + (2 * n - 4 + k) * GROUP + place), 2)]
+                    slot = bb_late.at[pl.ds(2 * (LATE_TILES * lev + (2 * n - 2 * EARLY + k) * GROUP + place), 2)]
                     remote(source, slot, bwd_send, bwd_recv.at[1], wide=member_at, level=1 - lev).start()
                 else:
                     slot = bb.at[pl.ds(2 * ((2 * n + k) * GROUP + place), 2)]
@@ -358,14 +366,15 @@
             lax.fori_loop(1 if late and offsets[k] == 0 else 0, GROUP, send, 0)
 
     def adjoint_far(n, _):
-        adjoint_pair(n, (2 - n, 6 - n), False)
+        a = 2 - n + 3 * (n // 2)
+        adjoint_pair(n, (a, 8 - a), False)
         return _
 
-    lax.fori_loop(0, 2, adjoint_far, 0)
-    adjoint_pair(2, (3, 7), True)
-    adjoint_pair(3, (4, 0), True)
+    lax.fori_loop(0, EARLY, adjoint_far, 0)
+    for n in range(EARLY, 4):
+        adjoint_pair(n, PAIRS[n], True)
     mine = pl.ds(2 * w, 2)
-    slot = pl.ds(2 * (64 * lev + 3 * GROUP + place), 2)
+    slot = pl.ds(2 * (LATE_TILES * lev + (7 - 2 * EARLY) * GROUP + place), 2)
     remote(sb.at[mine], bb_late.at[slot], bwd_send, bwd_recv.at[1], level=1 - lev).start()
     pltpu.make_async_copy(sb.at[mine], bb_late.at[slot], bwd_recv.at[1]).start()
 
@@ -387,7 +396,7 @@
 
     def half_gradient():
         wait_bytes(bb, bwd_recv.at[0])
-        half[...] = rows_adjoint(bb[...], (2, 6, 1, 5))
+        half[...] = rows_adjoint(bb[...], [i for pair in PAIRS[:EARLY] for i in pair])
         half_copy.start()
 
     half_copy = remote(half, twin, half_send, half_recv, level=1 - lev)
@@ -401,7 +410,9 @@
     sg_out.start()
 
     wait_bytes(bb_late, bwd_recv.at[1])
-    rows_done = half[...] + rows_adjoint(bb_late[0:128] + bb_late[128:256], (3, 7, 4, 0))
+    rows_done = half[...] + rows_adjoint(
+        bb_late[0 : 2 * LATE_TILES] + bb_late[2 * LATE_TILES :], [i for pair in PAIRS[EARLY:] for i in pair]
+    )
     half_copy.wait_recv()
     mgb[...] = mc[...] + lax.dot_general(
         rows_done + twin[...], cf[...], (((1,), (1,)), ((), ())), precision=PRECISE, preferred_element_type=F32
@@ -410,7 +421,7 @@
     mg_out.start()
 
     wait_bytes(ext.at[pl.ds(0, 254)], fwd_send)
-    wait_bytes(nat_s.at[pl.ds(0, 2 * 192 - 2)], bwd_send)
+    wait_bytes(nat_s.at[pl.ds(0, 2 * (WIDE + LATE_TILES) - 2)], bwd_send)
     for copy in lev_copies + static_rows + weighted_rows + [half_copy]:
         copy.wait_send()
     inc_out.wait()
@@ -462,7 +473,7 @@
         scratch_shapes=[
             vmem(WIDE, LEVELS, 8, 1024, dtype=BF16),
             vmem(128, 128), vmem(128, 128), vmem(256, 128),
-            vmem(256, 128), vmem(256, 128), vmem(128, 128), vmem(256, 128),
+            vmem(256, 128), vmem(256, 128), vmem(64 * EARLY, 128), vmem(256, 128),
             vmem(512, 128), vmem(512, 128), vmem(512, 128),
             vmem(OWN, 128), vmem(64, 128, dtype=jnp.int32), vmem(8, 128, dtype=jnp.int32),
             vmem(8, 128, dtype=jnp.int32),
@@ -474,7 +485,7 @@
             vmem(LEVELS, 8, 1024), vmem(LEVELS, 8, 1024), vmem(16, 1024),
             vmem(OWN, 128), vmem(OWN, 128), vmem(128, 128),
             vmem(2 * PACKED, 128), vmem(PACKED, 128), vmem(2 * PACKED, 128), vmem(PACKED, 128),
-            vmem(128, 128), vmem(128, 128), vmem(WIDE, 1024), vmem(256, 128),
+            vmem(128, 128), vmem(128, 128), vmem(WIDE, 1024), vmem(4 * LATE_TILES, 128),
             dma((10,)), dma((3,)), dma, dma((8,)), dma, dma((2,)), dma((3,)), dma((3,)), dma((12,)), dma((12,)), dma, dma,
         ],
         compiler_params=pltpu.CompilerParams(

time: 45 us -> 44.7 us (level)
  no operation moved by 1% of the time
where the time goes in v4:
time: 44.7 us; the launch traced here: 44.6 us
  Pallas kernels  43.9 us (98%)
  between operations  0.64 us (1%)
    pallas_call x1, Pallas kernels, on_device(): pl.pallas_call(kernel, out_shape=(jax.ShapeDtypeStruct((OWN, 128), F32),...  42.2 us
    pallas_call x1, Pallas kernels, on_device(): pl.pallas_call(finish, out_shape=(jax.ShapeDtypeStruct((OWN, 128), F32),...  1.71 us

profile of v4, /device:TPU:1, one launch (start us, length us, event | category | flops | bytes accessed | tf_op | source)
XLA Modules:
  0.0 44.6 jit_solution(6150792058798099942)
XLA Ops:
  0.6 42.2 %increment_and_gradients.1 = (f32[256,128]{1,0:T(8,128)}, f32[128,128]{1,0:T(8,128)}, f32[256,128]{1,0:T(8,128)}) custom-call(f32[128,128]{1,0:T(8,128)} %bitcast.37, f32[256,128]{1,0:T(8,128)} %bitcast.34, bf16[128,4,8,1024]{3,2,1,0:T(8,128)(2,1)} %pert_hbm.1, f32[256,128]{1,0:T(8,128)} %bitcast.35, f32[256,128]{1,0:T(8,128)} %bitcast.36, ...), custom_call_target="tpu_custom_call" | custom-call | tf_op jit(solution)/shard_map/increment_and_gradients/pallas_call | solution.py:464
  42.9 1.7 %finish.1 = (f32[256,128]{1,0:T(8,128)}, f32[128,128]{1,0:T(8,128)}, f32[256,128]{1,0:T(8,128)}) custom-call(f32[256,128]{1,0:T(8,128)} %get-tuple-element.9.refs_0_, f32[128,128]{1,0:T(8,128)} %get-tuple-element.10.refs_1_, f32[256,128]{1,0:T(8,128)} %get-tuple-element.11.refs_2_), custom_call_target="tpu_custom_call" | custom-call | tf_op jit(solution)/shard_map/finish/pallas_call | solution.py:507
